TPU v7x, 128 devices: a whole 4x4x4 slice. The times are simulated.
128 devices in a mesh: dp: 16 (over y, x), seq: 8 (over z, core).
Axes of the slice: x: 4, y: 4, z: 4, core: 2. Of those that a mesh axis runs over, the one named last changes fastest.
Arguments:
- tokens_in: bfloat16 [16, 4096, 1024], P('dp', 'seq'), may hold values from -6 to 6
- user_ids: int32 [16, 4096], P('dp'), may hold values from 0 to 3, never falling along the last dimension, each value on 1 to 2048 neighbouring positions
- w_in: bfloat16 [1024, 2048], replicated, may hold values from -0.1875 to 0.1875
- w_out: bfloat16 [512, 1024], replicated, may hold values from -0.25 to 0.25
- cotangent: bfloat16 [16, 4096, 1024], P('dp', 'seq'), may hold values from -6 to 6
Outputs:
- output: bfloat16 [16, 4096, 1024], P('dp', 'seq')
- grad_tokens: bfloat16 [16, 4096, 1024], P('dp', 'seq')
- grad_w_in: float32 [1024, 2048], P(('dp', 'seq'))
- grad_w_out: float32 [512, 1024], P(None, ('dp', 'seq'))
Inputs may be any that keep to these rules, and one draw needn't show every extreme that they name: `user_ids`: in each stream the user number never falls; each user holds 1 to 2048 consecutive events and some user holds exactly 2048.
All inputs are finite; a program needn't handle non-finite values.
Results may differ from a plain program's by a relative error of at most 0.015.
Values may be sent and summed in bfloat16 or wider, within the bound.
A program may use at most 128 MiB of HBM per device.

v0:
```python
import math

import jax
import jax.numpy as jnp
from jax import lax
from jax.sharding import PartitionSpec as P

HEADS = 4
HD = 128


epsilon = 1e-05


def from_behind(value, axis, by):
    devices = lax.axis_size(axis)
    pairs = [(i, i + by) for i in range(devices) if 0 <= i + by < devices]
    return lax.ppermute(value, axis, pairs)


def normalize(values):
    center = values - jnp.mean(values, axis=-1, keepdims=True)
    inverse = lax.rsqrt(jnp.mean(center * center, axis=-1, keepdims=True) + epsilon)
    return center * inverse


def norm_back(values, upstream):
    center = values - jnp.mean(values, axis=-1, keepdims=True)
    inverse = lax.rsqrt(jnp.mean(center * center, axis=-1, keepdims=True) + epsilon)
    scaled = center * inverse
    return inverse * (
        upstream
        - jnp.mean(upstream, axis=-1, keepdims=True)
        - scaled * jnp.mean(upstream * scaled, axis=-1, keepdims=True)
    )


def silu_slope(values):
    sigma = jax.nn.sigmoid(values)
    return sigma * (1.0 + values * (1.0 - sigma))


def local(tokens_in, user_ids, w_in, w_out, cotangent):
    tokens = tokens_in[0]
    id_table = user_ids[0]
    upstream = cotangent[0]
    n_rows = tokens.shape[0]
    width = w_out.shape[0]
    span = lax.axis_size("seq") // 2
    q_start = lax.axis_index("seq") * n_rows
    scale = 1.0 / math.sqrt(HD)
    tokens_f = tokens.astype(jnp.float32)
    normed = normalize(tokens_f).astype(jnp.bfloat16)
    hidden = jnp.dot(normed, w_in, preferred_element_type=jnp.float32)
    active = jax.nn.silu(hidden).astype(jnp.bfloat16)
    gate_u = active[:, :width]
    values_own = active[:, width : 2 * width]
    query = active[:, 2 * width : 3 * width]
    keys_own = active[:, 3 * width :]
    query_heads = query.reshape(n_rows, HEADS, HD)
    my_users = lax.dynamic_slice_in_dim(id_table, q_start, n_rows)
    q_pos = q_start + jnp.arange(n_rows, dtype=jnp.int32)

    def key_mask(start):
        k_pos = start + jnp.arange(n_rows, dtype=jnp.int32)
        k_users = lax.dynamic_slice_in_dim(id_table, jnp.maximum(start, 0), n_rows)
        allowed = (
            (k_pos[None, :] >= 0)
            & (k_users[None, :] == my_users[:, None])
            & (k_pos[None, :] <= q_pos[:, None])
        )
        return allowed.astype(jnp.float32)[None]

    pieces = []
    pieces.append((keys_own, values_own, q_start))
    for distance in range(1, span + 1):
        keys_far, values_far = from_behind((keys_own, values_own), "seq", distance)
        pieces.append((keys_far, values_far, q_start - distance * n_rows))
    attended = jnp.zeros((n_rows, HEADS, HD), jnp.float32)
    for piece_keys, piece_values, start in pieces:
        key_heads = piece_keys.reshape(n_rows, HEADS, HD)
        value_heads = piece_values.reshape(n_rows, HEADS, HD)
        scores = (
            jnp.einsum("qhd,khd->hqk", query_heads, key_heads, preferred_element_type=jnp.float32)
            * scale
        )
        weights = (jax.nn.silu(scores) * key_mask(start)).astype(jnp.bfloat16)
        attended = attended + jnp.einsum(
            "hqk,khd->qhd", weights, value_heads, preferred_element_type=jnp.float32
        )
    attended = attended.reshape(n_rows, width)
    normed_out = normalize(attended)
    gated = (normed_out * gate_u.astype(jnp.float32)).astype(jnp.bfloat16)
    output = (jnp.dot(gated, w_out, preferred_element_type=jnp.float32) + tokens_f).astype(
        jnp.bfloat16
    )
    grad_w_out = jnp.dot(gated.T, upstream, preferred_element_type=jnp.float32)
    grad_gated = jnp.dot(upstream, w_out.T, preferred_element_type=jnp.float32)
    grad_u = grad_gated * normed_out
    grad_normed = grad_gated * gate_u.astype(jnp.float32)
    grad_attended = norm_back(attended, grad_normed).astype(jnp.bfloat16)
    grad_heads = grad_attended.reshape(n_rows, HEADS, HD)
    grad_query = jnp.zeros((n_rows, HEADS, HD), jnp.float32)
    key_terms = []
    for piece_keys, piece_values, start in pieces:
        key_heads = piece_keys.reshape(n_rows, HEADS, HD)
        value_heads = piece_values.reshape(n_rows, HEADS, HD)
        mask = key_mask(start)
        scores = (
            jnp.einsum("qhd,khd->hqk", query_heads, key_heads, preferred_element_type=jnp.float32)
            * scale
        )
        weights = (jax.nn.silu(scores) * mask).astype(jnp.bfloat16)
        part_values = jnp.einsum(
            "hqk,qhd->khd", weights, grad_heads, preferred_element_type=jnp.float32
        )
        grad_weights = jnp.einsum(
            "qhd,khd->hqk", grad_heads, value_heads, preferred_element_type=jnp.float32
        )
        grad_scores = (grad_weights * silu_slope(scores) * mask).astype(jnp.bfloat16)
        grad_query = (
            grad_query
            + jnp.einsum("hqk,khd->qhd", grad_scores, key_heads, preferred_element_type=jnp.float32)
            * scale
        )
        part_keys = (
            jnp.einsum("hqk,qhd->khd", grad_scores, query_heads, preferred_element_type=jnp.float32)
            * scale
        )
        key_terms.append(
            (part_keys.reshape(n_rows, width), part_values.reshape(n_rows, width), start)
        )
    grad_keys = key_terms[0][0]
    grad_values = key_terms[0][1]
    for distance in range(1, span + 1):
        back_keys, back_values = (
            from_behind(key_terms[distance][0].astype(jnp.bfloat16), "seq", -distance).astype(
                jnp.float32
            ),
            from_behind(key_terms[distance][1].astype(jnp.bfloat16), "seq", -distance).astype(
                jnp.float32
            ),
        )
        grad_keys = grad_keys + back_keys
        grad_values = grad_values + back_values
    grad_all = jnp.concatenate(
        [grad_u, grad_values, grad_query.reshape(n_rows, width), grad_keys], axis=1
    )
    grad_hidden = (grad_all * silu_slope(hidden)).astype(jnp.bfloat16)
    grad_w_in = jnp.dot(normed.T, grad_hidden, preferred_element_type=jnp.float32)
    grad_normed_in = jnp.dot(grad_hidden, w_in.T, preferred_element_type=jnp.float32)
    grad_tokens = (norm_back(tokens_f, grad_normed_in) + upstream.astype(jnp.float32)).astype(
        jnp.bfloat16
    )
    total_in, total_out = (
        lax.psum_scatter(grad_w_in, ("dp", "seq"), scatter_dimension=0, tiled=True),
        lax.psum_scatter(grad_w_out, ("dp", "seq"), scatter_dimension=1, tiled=True),
    )
    return (output[None], grad_tokens[None], total_in, total_out)


def solution(mesh):
    in_specs = (P("dp", "seq", None), P("dp", None), P(), P(), P("dp", "seq", None))
    out_specs = (
        P("dp", "seq", None),
        P("dp", "seq", None),
        P(("dp", "seq"), None),
        P(None, ("dp", "seq")),
    )
    return jax.shard_map(local, mesh=mesh, in_specs=in_specs, out_specs=out_specs, check_vma=False)
```

profile of v0, /device:TPU:0, one launch (start us, length us, event | category | flops | bytes accessed | tf_op | source)
XLA Modules:
  0.0 1482.3 jit_solution(18436589373716127923)
XLA Ops:
  10.4 7.3 multiply_convert_fusion.10
  20.2 6.7 collective-permute-start.7
  26.9 2.9 collective-permute-start.5
  29.8 2.9 collective-permute-start.3
  38.6 3.4 and_convert_fusion.2
  42.0 3.6 multiply_convert_fusion.9
  56.1 5.1 collective-permute-done.3
  61.3 11.2 collective-permute-start.6
  76.6 5.0 multiply_convert_fusion.6
  81.5 2.2 fusion.49
  83.8 3.6 multiply_convert_fusion.5
  87.4 7.6 collective-permute-done.6
  96.9 3.6 multiply_convert_fusion.8
  100.5 2.4 convolution_add_fusion.3
  102.9 3.5 multiply_convert_fusion.7
  111.2 2.8 fusion.69
  114.0 2.8 fusion.34
  123.8 3.2 multiply_convert_fusion.1
  130.1 3.2 multiply_convert_fusion
  140.4 3.1 multiply_convert_fusion.2
  155.2 3.1 fusion.27
  158.6 4.0 multiply_convert_fusion.3
  167.0 2.2 copy.66
  179.1 4.1 fusion.18
  189.6 2.6 copy.70
  192.2 2.3 convert_add_fusion
  194.6 14.0 collective-permute-done.11
  209.7 2.5 collective-permute-done.9
  217.0 5.8 fusion.80
  225.5 5.4 fusion.84
  232.8 588.3 %reduce-scatter.5.cloned.1.call-done = f32[512,8]{0,1:T(8,128)} async-done(((f32[512,1024]{0,1:T(8,128)}), f32[512,8]{0,1:T(8,128)}) %reduce-scatter.5.cloned.1.call-update) | async-done | bytes 16400 | tf_op jit(solution)/shard_map/reduce_scatter | solution.py:157
  821.1 653.9 %reduce-scatter.3.cloned.1.call-done = f32[8,2048]{1,0:T(8,128)} async-done(((f32[1024,2048]{1,0:T(8,128)}), f32[8,2048]{1,0:T(8,128)}) %reduce-scatter.3.cloned.1.call-update) | async-done | bytes 65552 | tf_op jit(solution)/shard_map/reduce_scatter | solution.py:156
  (187 shorter events, 92.9 us)
Async XLA Ops:
  7.2 104.0 %copy-start = (bf16[512,1024]{1,0:T(8,128)(2,1)S(1)}, bf16[512,1024]{1,0:T(8,128)(2,1)}, u32[]{:S(2)}) copy-start(bf16[512,1024]{1,0:T(8,128)(2,1)} %param.8) | copy-start | bytes 3145732
  7.2 813.9 %reduce-scatter.5.cloned.1.call-start = ((), (), s32[]{:S(2)}) async-start(), calls=%async_computation.3 | async-start | bytes 2113536 | tf_op jit(solution)/shard_map/reduce_scatter | solution.py:157
  17.7 20.8 %copy-start.46 = (s32[1,4096]{1,0:T(1,128)S(1)}, s32[1,4096]{1,0:T(1,128)}, u32[]{:S(2)}) copy-start(s32[1,4096]{1,0:T(1,128)} %param.6) | copy-start | bytes 49156
  20.2 27.6 %collective-permute-start.7 = (bf16[512,512]{1,0:T(8,128)(2,1)}, bf16[512,512]{1,0:T(8,128)(2,1)}, u32[]{:S(2)}, u32[]{:S(2)}) collective-permute-start(bf16[512,512]{1,0:T(8,128)(2,1)} %get-tuple-element.12), channel_id=1, source_target_pairs={{0,4},{1,5},{2,6},{3,7},{8,12},{9,13},{10,14},{11,15},{16,20},{17,... | collective-permute-start | bytes 1572872 | tf_op jit(solution)/shard_map/ppermute | solution.py:18
  26.9 25.0 %collective-permute-start.5 = (bf16[512,512]{1,0:T(8,128)(2,1)}, bf16[512,512]{1,0:T(8,128)(2,1)}, u32[]{:S(2)}, u32[]{:S(2)}) collective-permute-start(bf16[512,512]{1,0:T(8,128)(2,1)} %get-tuple-element.12), channel_id=1, source_target_pairs={{0,3},{1,4},{2,5},{3,6},{4,7},{8,11},{9,12},{10,13},{11,14},{12,15... | collective-permute-start | bytes 1572872 | tf_op jit(solution)/shard_map/ppermute | solution.py:18
  29.8 31.4 %collective-permute-start.3 = (bf16[512,512]{1,0:T(8,128)(2,1)}, bf16[512,512]{1,0:T(8,128)(2,1)}, u32[]{:S(2)}, u32[]{:S(2)}) collective-permute-start(bf16[512,512]{1,0:T(8,128)(2,1)} %get-tuple-element.12), channel_id=1, source_target_pairs={{0,2},{1,3},{2,4},{3,5},{4,6},{5,7},{8,10},{9,11},{10,12},{11,13},... | collective-permute-start | bytes 1572872 | tf_op jit(solution)/shard_map/ppermute | solution.py:18
  32.7 41.8 %collective-permute-start.1 = (bf16[512,512]{1,0:T(8,128)(2,1)}, bf16[512,512]{1,0:T(8,128)(2,1)}, u32[]{:S(2)}, u32[]{:S(2)}) collective-permute-start(bf16[512,512]{1,0:T(8,128)(2,1)} %get-tuple-element.12), channel_id=1, source_target_pairs={{0,1},{1,2},{2,3},{3,4},{4,5},{5,6},{6,7},{8,9},{9,10},{10,11},{11... | collective-permute-start | bytes 1572872 | tf_op jit(solution)/shard_map/ppermute | solution.py:18
  34.8 46.7 %collective-permute-start.4 = (bf16[512,512]{1,0:T(8,128)(2,1)}, bf16[512,512]{1,0:T(8,128)(2,1)}, u32[]{:S(2)}, u32[]{:S(2)}) collective-permute-start(bf16[512,512]{1,0:T(8,128)(2,1)} %get-tuple-element.14), channel_id=1, source_target_pairs={{0,3},{1,4},{2,5},{3,6},{4,7},{8,11},{9,12},{10,13},{11,14},{12,15... | collective-permute-start | bytes 1572872 | tf_op jit(solution)/shard_map/ppermute | solution.py:18
  47.8 58.6 %collective-permute-start.2 = (bf16[512,512]{1,0:T(8,128)(2,1)}, bf16[512,512]{1,0:T(8,128)(2,1)}, u32[]{:S(2)}, u32[]{:S(2)}) collective-permute-start(bf16[512,512]{1,0:T(8,128)(2,1)} %get-tuple-element.14), channel_id=1, source_target_pairs={{0,2},{1,3},{2,4},{3,5},{4,6},{5,7},{8,10},{9,11},{10,12},{11,13},... | collective-permute-start | bytes 1572872 | tf_op jit(solution)/shard_map/ppermute | solution.py:18
  52.0 48.5 %collective-permute-start = (bf16[512,512]{1,0:T(8,128)(2,1)}, bf16[512,512]{1,0:T(8,128)(2,1)}, u32[]{:S(2)}, u32[]{:S(2)}) collective-permute-start(bf16[512,512]{1,0:T(8,128)(2,1)} %get-tuple-element.14), channel_id=1, source_target_pairs={{0,1},{1,2},{2,3},{3,4},{4,5},{5,6},{6,7},{8,9},{9,10},{10,11},{11... | collective-permute-start | bytes 1572872 | tf_op jit(solution)/shard_map/ppermute | solution.py:18
  61.3 33.7 %collective-permute-start.6 = (bf16[512,512]{1,0:T(8,128)(2,1)}, bf16[512,512]{1,0:T(8,128)(2,1)}, u32[]{:S(2)}, u32[]{:S(2)}) collective-permute-start(bf16[512,512]{1,0:T(8,128)(2,1)} %get-tuple-element.14), channel_id=1, source_target_pairs={{0,4},{1,5},{2,6},{3,7},{8,12},{9,13},{10,14},{11,15},{16,20},{17,... | collective-permute-start | bytes 1572872 | tf_op jit(solution)/shard_map/ppermute | solution.py:18
  83.8 13.0 copy-start.30
  83.8 13.0 copy-start.37
  87.4 13.1 copy-start.8
  143.5 11.6 copy-start.15
  151.3 32.0 %collective-permute-start.14 = (bf16[512,512]{1,0:T(8,128)(2,1)}, bf16[512,512]{1,0:T(8,128)(2,1)}, u32[]{:S(2)}, u32[]{:S(2)}) collective-permute-start(bf16[512,512]{1,0:T(8,128)(2,1)} %copy.74), channel_id=1, source_target_pairs={{3,0},{4,1},{5,2},{6,3},{7,4},{11,8},{12,9},{13,10},{14,11},{15,12... | collective-permute-start | bytes 1572872 | tf_op jit(solution)/shard_map/ppermute | solution.py:18
  152.6 32.7 %collective-permute-start.15 = (bf16[512,512]{1,0:T(8,128)(2,1)}, bf16[512,512]{1,0:T(8,128)(2,1)}, u32[]{:S(2)}, u32[]{:S(2)}) collective-permute-start(bf16[512,512]{1,0:T(8,128)(2,1)} %copy.75), channel_id=1, source_target_pairs={{4,0},{5,1},{6,2},{7,3},{12,8},{13,9},{14,10},{15,11},{20,16},{21,... | collective-permute-start | bytes 1572872 | tf_op jit(solution)/shard_map/ppermute | solution.py:18
  153.9 32.6 %collective-permute-start.13 = (bf16[512,512]{1,0:T(8,128)(2,1)}, bf16[512,512]{1,0:T(8,128)(2,1)}, u32[]{:S(2)}, u32[]{:S(2)}) collective-permute-start(bf16[512,512]{1,0:T(8,128)(2,1)} %copy.73), channel_id=1, source_target_pairs={{2,0},{3,1},{4,2},{5,3},{6,4},{7,5},{10,8},{11,9},{12,10},{13,11},... | collective-permute-start | bytes 1572872 | tf_op jit(solution)/shard_map/ppermute | solution.py:18
  158.3 1316.7 %reduce-scatter.3.cloned.1.call-start = ((), (), s32[]{:S(2)}) async-start(), calls=%async_computation.2 | async-start | bytes 8454144 | tf_op jit(solution)/shard_map/reduce_scatter | solution.py:156
  164.4 8.9 copy-start.35
  167.0 12.1 copy-start.21
  174.3 12.2 copy-start.45
  176.4 11.4 copy-start.5
  176.4 15.8 %collective-permute-start.12 = (bf16[512,512]{1,0:T(8,128)(2,1)}, bf16[512,512]{1,0:T(8,128)(2,1)}, u32[]{:S(2)}, u32[]{:S(2)}) collective-permute-start(bf16[512,512]{1,0:T(8,128)(2,1)} %copy.72), channel_id=1, source_target_pairs={{1,0},{2,1},{3,2},{4,3},{5,4},{6,5},{7,6},{9,8},{10,9},{11,10},{12... | collective-permute-start | bytes 1572872 | tf_op jit(solution)/shard_map/ppermute | solution.py:18
  177.8 30.7 %collective-permute-start.11 = (bf16[512,512]{1,0:T(8,128)(2,1)}, bf16[512,512]{1,0:T(8,128)(2,1)}, u32[]{:S(2)}, u32[]{:S(2)}) collective-permute-start(bf16[512,512]{1,0:T(8,128)(2,1)} %copy.69), channel_id=1, source_target_pairs={{4,0},{5,1},{6,2},{7,3},{12,8},{13,9},{14,10},{15,11},{20,16},{21,... | collective-permute-start | bytes 1572872 | tf_op jit(solution)/shard_map/ppermute | solution.py:18
  183.3 26.5 %collective-permute-start.10 = (bf16[512,512]{1,0:T(8,128)(2,1)}, bf16[512,512]{1,0:T(8,128)(2,1)}, u32[]{:S(2)}, u32[]{:S(2)}) collective-permute-start(bf16[512,512]{1,0:T(8,128)(2,1)} %copy.68), channel_id=1, source_target_pairs={{3,0},{4,1},{5,2},{6,3},{7,4},{11,8},{12,9},{13,10},{14,11},{15,12... | collective-permute-start | bytes 1572872 | tf_op jit(solution)/shard_map/ppermute | solution.py:18
  185.2 27.0 %collective-permute-start.9 = (bf16[512,512]{1,0:T(8,128)(2,1)}, bf16[512,512]{1,0:T(8,128)(2,1)}, u32[]{:S(2)}, u32[]{:S(2)}) collective-permute-start(bf16[512,512]{1,0:T(8,128)(2,1)} %copy.67), channel_id=1, source_target_pairs={{2,0},{3,1},{4,2},{5,3},{6,4},{7,5},{10,8},{11,9},{12,10},{13,11},... | collective-permute-start | bytes 1572872 | tf_op jit(solution)/shard_map/ppermute | solution.py:18
  186.5 25.7 %collective-permute-start.8 = (bf16[512,512]{1,0:T(8,128)(2,1)S(1)}, bf16[512,512]{1,0:T(8,128)(2,1)}, u32[]{:S(2)}, u32[]{:S(2)}) collective-permute-start(bf16[512,512]{1,0:T(8,128)(2,1)S(1)} %copy-done.45), channel_id=1, source_target_pairs={{1,0},{2,1},{3,2},{4,3},{5,4},{6,5},{7,6},{9,8},{10,9},{11,10},{12... | collective-permute-start | bytes 1572872 | tf_op jit(solution)/shard_map/ppermute | solution.py:18
  189.6 22.6 %copy-start.23 = (f32[512,512]{1,0:T(8,128)S(1)}, f32[512,512]{1,0:T(8,128)}, u32[]{:S(2)}) copy-start(f32[512,512]{1,0:T(8,128)} %copy.65) | copy-start | bytes 3145732
  192.2 21.9 %copy-start.18 = (f32[512,512]{1,0:T(8,128)S(1)}, f32[512,512]{1,0:T(8,128)}, u32[]{:S(2)}) copy-start(f32[512,512]{1,0:T(8,128)} %copy.70) | copy-start | bytes 3145732
  192.2 21.9 %copy-start.19 = (f32[512,2048]{1,0:T(8,128)S(1)}, f32[512,2048]{1,0:T(8,128)}, u32[]{:S(2)}) copy-start(f32[512,2048]{1,0:T(8,128)} %get-tuple-element.27) | copy-start | bytes 12582916
  192.2 21.9 %copy-start.20 = (f32[512,512]{1,0:T(8,128)S(1)}, f32[512,512]{1,0:T(8,128)}, u32[]{:S(2)}) copy-start(f32[512,512]{1,0:T(8,128)} %get-tuple-element.10) | copy-start | bytes 3145732
  (37 other events, 135.0 us)
Sparse Core Ops, SparseCore 0:
  158.4 662.6 reduce-scatter.4
  824.0 650.9 reduce-scatter.2
where the time goes:
time: 1490 us; the launch traced here: 1480 us
  waiting for transfers between devices  1270 us (85%)
  matrix products  93.9 us (6%)
  starting transfers between devices  42.8 us (3%)
  local copies, waits for them, and re-layouts  40 us (3%)
  other arithmetic  17.2 us (1%)
  between operations  15.1 us (1%)
    reduce_scatter x1, waiting for transfers between devices, local(): lax.psum_scatter(grad_w_in, ('dp', 'seq'), scatter_dimension=0, tiled=True)  654 us
    reduce_scatter x1, waiting for transfers between devices, local(): lax.psum_scatter(grad_w_out, ('dp', 'seq'), scatter_dimension=1, tiled=True)  588 us
    ppermute x16, starting transfers between devices, from_behind(): return lax.ppermute(value, axis, pairs)  42.4 us
    ppermute x16, waiting for transfers between devices, from_behind(): return lax.ppermute(value, axis, pairs)  31 us
  transfers between devices with their start and end apart: 18, of which 8 were waited for; matrix products, arithmetic and copies ran while one was open for 6% of the time, Pallas kernels for 0%

commit v1 on v0

v1 whole, which is shorter than its diff:
```python
import math

import jax
import jax.numpy as jnp
from jax import lax
from jax.experimental import pallas as pl
from jax.experimental.pallas import tpu as pltpu
from jax.sharding import PartitionSpec as P

HEADS = 4
HD = 128
ROWS = 512
F32 = jnp.float32
BF16 = jnp.bfloat16
EPS = 1e-05
HALF_SCALE = 0.5 / math.sqrt(HD)
MESH = pl.DeviceIdType.MESH
NB = 5

OWN_MOVES = (
    (0, 1, 0, (0, 1, 2, 3)),
    (0, 3, 0, (2, 3)),
    (1, 2, 1, (0, 1, 2)),
    (1, 0, 1, (3, 1, 2)),
    (2, 3, 2, (0, 1, 2, 3)),
)
RELAYS = {
    (1, 0, 0): 2, (1, 0, 1): 2,
    (0, 1, 3): 3, (0, 1, 1): 3, (0, 1, 2): 3,
    (3, 0, 2): 2, (3, 0, 3): 2, (3, 1, 3): 2,
    (2, 1, 0): 3,
}
ARRIVALS = {
    0: ((1, 3), (1, 1), (1, 2)),
    1: ((0, 0), (0, 1), (0, 2), (0, 3)),
    2: ((1, 0), (1, 1), (0, 2), (1, 2), (0, 3), (0, 0), (1, 3), (0, 1)),
    3: ((2, 0), (0, 2), (2, 1), (0, 3), (2, 2), (1, 3), (2, 3), (1, 1), (1, 2), (1, 0)),
}
STEPS = 10


def place():
    dp, seq = lax.axis_index("dp"), lax.axis_index("seq")
    return dp // 4, dp % 4, seq // 2, seq % 2


def device(y, x, z, core):
    return {"dp": y * 4 + x, "seq": z * 2 + core}


def turn(i, d):
    return lax.rem(i + d, 4)


def remote(src, dst, send, recv, target):
    return pltpu.make_async_remote_copy(
        src_ref=src, dst_ref=dst, send_sem=send, recv_sem=recv,
        device_id=target, device_id_type=MESH)


def dot_nn(a, b):
    return jnp.dot(a, b, preferred_element_type=F32)


def dot_nt(a, b):
    return lax.dot_general(a, b, (((1,), (1,)), ((), ())), preferred_element_type=F32)


def dot_tn(a, b):
    return lax.dot_general(a, b, (((0,), (0,)), ((), ())), preferred_element_type=F32)


class Gather:
    def __init__(self, near, far, sems, chip, core, target):
        self.near, self.far = near, far
        self.ss, self.rs, self.sp, self.rp = sems
        self.chip, self.core, self.target = chip, core, target

    def move(self, sender, receiver, owner, h):
        k = 0 if receiver == sender + 1 else 1
        return remote(self.near.at[owner, h], self.near.at[owner, h], self.ss.at[owner, h, k],
                      self.rs.at[owner, h], self.target(receiver, self.core))

    def share(self, owner, h):
        return remote(self.near.at[owner, h], self.far.at[owner, h], self.sp.at[owner, h],
                      self.rp.at[owner, h], self.target(self.chip, 1 - self.core))

    def start(self):
        @pl.when(self.core == 0)
        def _():
            for h in range(HEADS):
                self.share(self.chip, h).start()
        for sender, receiver, owner, heads in OWN_MOVES:
            @pl.when(self.chip == sender)
            def _():
                for h in heads:
                    self.move(sender, receiver, owner, h).start()

    def arrive(self, step):
        for role, order in ARRIVALS.items():
            if step >= len(order):
                continue
            owner, h = order[step]

            @pl.when(self.chip == role)
            def _():
                self.move(role, (role + 1) % 4, owner, h).wait_recv()
                if (role, owner, h) in RELAYS:
                    self.move(role, RELAYS[role, owner, h], owner, h).start()
                if owner == role - 1:
                    self.share(owner, h).start()
                if owner == role - 2:
                    @pl.when(self.core == 1)
                    def _():
                        self.share(owner, h).start()

    def drain(self):
        @pl.when(self.core == 0)
        def _():
            for h in range(HEADS):
                self.share(self.chip, h).wait_send()
        for sender, receiver, owner, heads in OWN_MOVES:
            @pl.when(self.chip == sender)
            def _():
                for h in heads:
                    self.move(sender, receiver, owner, h).wait_send()
        for (role, owner, h), receiver in RELAYS.items():
            @pl.when(self.chip == role)
            def _():
                self.move(role, receiver, owner, h).wait_send()
        for role, order in ARRIVALS.items():
            for owner, h in order:
                if owner == role - 1:
                    @pl.when(self.chip == role)
                    def _():
                        self.share(owner, h).wait_send()
                if owner == role - 2:
                    @pl.when((self.chip == role) & (self.core == 1))
                    def _():
                        self.share(owner, h).wait_send()

    def block(self, d):
        if d == 0:
            return self.near, self.chip
        if d % 2 == 0:
            return self.near, self.chip - d // 2
        return self.far, self.chip - (d + 1) // 2 + self.core

    def wait_share(self, d, h):
        if d % 2 == 1:
            owner = self.chip - (d + 1) // 2 + self.core
            self.share(owner, h).wait_recv()


def layer_kernel(tokens, ids, w_in, w_out, cot, output, grad_tokens, out_in, out_out,
                 normed, slope, u, kv, kv2, qs, qs2, gs, gs2, att, dq, dk, dv, gated, gh, masks, masks_t,
                 tmp, part, s2, recv1, r2a, r2b, s3a, s3b, r3a, r3b, t4, r4,
                 kss, krs, ksp, krp, qss, qrs, qsp, qrp, gss, grs, gsp, grp,
                 ss1, rs1, ss2, rs2, ss3, rs3, ss4, rs4):
    y, x, z, c = place()
    other = 1 - c
    block = z * 2 + c
    peers = ([device(y, x, z, other)]
             + [device(y, turn(x, d), z, c) for d in (1, 2, 3)]
             + [device(turn(y, d), x, z, c) for d in (1, 2, 3)]
             + [device(y, x, turn(z, d), c) for d in (1, 2, 3)])
    barrier = pltpu.get_barrier_semaphore()
    for t in peers:
        pl.semaphore_signal(barrier, inc=1, device_id=t, device_id_type=MESH)

    before = Gather(kv, kv2, (kss, krs, ksp, krp), z, c, lambda zz, cc: device(y, x, zz, cc))
    mz, mc = 3 - z, 1 - c

    def mirrored(zz, cc):
        return device(y, x, 3 - zz, 1 - cc)

    queries = Gather(qs, qs2, (qss, qrs, qsp, qrp), mz, mc, mirrored)
    grads = Gather(gs, gs2, (gss, grs, gsp, grp), mz, mc, mirrored)

    def stats(v):
        center = v - jnp.mean(v, axis=-1, keepdims=True)
        inverse = lax.rsqrt(jnp.mean(center * center, axis=-1, keepdims=True) + EPS)
        return center * inverse, inverse

    def row_loop(size):
        def wrap(body):
            @pl.loop(0, ROWS // size)
            def _(i):
                body(pl.ds(pl.multiple_of(i * size, size), size))
        return wrap

    @row_loop(128)
    def _(rows):
        normed[rows, :] = stats(tokens[rows, :].astype(F32))[0].astype(BF16)

    def features(col, put):
        @row_loop(256)
        def _(rows):
            half = 0.5 * dot_nn(normed[rows, :], w_in[:, col:col + 512])
            t = jnp.tanh(half)
            slope[rows, col:col + 512] = 0.5 * (1.0 + t) * (1.0 + half * (1.0 - t))
            put(rows, (half * (1.0 + t)).astype(BF16))

    def put_k(rows, a):
        for h in range(HEADS):
            kv[z, h, rows, 0:128] = a[:, h * 128:(h + 1) * 128]

    def put_v(rows, a):
        for h in range(HEADS):
            kv[z, h, rows, 128:256] = a[:, h * 128:(h + 1) * 128]

    def put_q(rows, a):
        for h in range(HEADS):
            qs[mz, h, rows, :] = a[:, h * 128:(h + 1) * 128]

    def put_u(rows, a):
        u[rows, :] = a

    features(1536, put_k)
    features(512, put_v)
    pl.semaphore_wait(barrier, len(peers))
    before.start()
    features(1024, put_q)
    features(0, put_u)

    def ids_of(b):
        b = jnp.clip(b, 0, 7)
        return ids[:, pl.ds(pl.multiple_of(b * ROWS, ROWS), ROWS)].astype(F32)

    own_ids = jnp.transpose(jnp.broadcast_to(ids_of(block), (128, ROWS)))
    own_col = jnp.broadcast_to(own_ids[:, 0:1], (ROWS, ROWS))
    one, nil = jnp.ones((ROWS, ROWS), F32), jnp.zeros((ROWS, ROWS), F32)
    down = lax.broadcasted_iota(jnp.int32, (ROWS, ROWS), 0)
    right = lax.broadcasted_iota(jnp.int32, (ROWS, ROWS), 1)
    for d in range(5):
        same = own_col == jnp.broadcast_to(ids_of(block - d), (ROWS, ROWS))
        same_t = own_col == jnp.broadcast_to(ids_of(block + d), (ROWS, ROWS))
        if d == 0:
            same = same & (right <= down)
            same_t = same_t & (down <= right)
        masks[d] = jnp.where(same, one, nil).astype(BF16)
        masks_t[d] = jnp.where(same_t, one, nil).astype(BF16)

    def spans(d, flip):
        if d == 0:
            pair = ((0, 256), (0, 512)) if not flip else ((0, 512), (256, 512))
        elif d == 4:
            pair = ((0, 512), (256, 512)) if not flip else ((0, 256), (0, 512))
        else:
            pair = ((0, 512), (0, 512))
        return ((0, 256) + pair[0], (256, 512) + pair[1])

    def forward(d):
        @pl.when(block >= d)
        def _():
            ref, i = before.block(d)

            @pl.loop(0, HEADS)
            def _(h):
                before.wait_share(d, h)
                for r0, r1, c0, c1 in spans(d, False):
                    half = dot_nt(qs[mz, h, r0:r1, :], ref[i, h, c0:c1, 0:128]) * HALF_SCALE
                    w = (half * (1.0 + jnp.tanh(half))).astype(BF16) * masks[d, r0:r1, c0:c1]
                    a = dot_nn(w, ref[i, h, c0:c1, 128:256])
                    if d == 0:
                        att[h, r0:r1, :] = a
                    else:
                        att[h, r0:r1, :] += a

    def query_back(d):
        @pl.when(block >= d)
        def _():
            ref, i = before.block(d)

            @pl.loop(0, HEADS)
            def _(h):
                for r0, r1, c0, c1 in spans(d, False):
                    half = dot_nt(qs[mz, h, r0:r1, :], ref[i, h, c0:c1, 0:128]) * HALF_SCALE
                    t = jnp.tanh(half)
                    dw = dot_nt(gs[mz, h, r0:r1, :], ref[i, h, c0:c1, 128:256])
                    ds = (dw * ((1.0 + t) * (1.0 + half * (1.0 - t)))).astype(BF16) * masks[d, r0:r1, c0:c1]
                    a = dot_nn(ds, ref[i, h, c0:c1, 0:128])
                    if d == 0:
                        dq[h, r0:r1, :] = a
                    else:
                        dq[h, r0:r1, :] += a

    def key_back(d):
        @pl.when(block + d <= 7)
        def _():
            qref, i = queries.block(d)
            gref, _ = grads.block(d)

            @pl.loop(0, HEADS)
            def _(h):
                queries.wait_share(d, h)
                grads.wait_share(d, h)
                for r0, r1, c0, c1 in spans(d, True):
                    qq, gg = qref[i, h, c0:c1, :], gref[i, h, c0:c1, :]
                    half = dot_nt(kv[z, h, r0:r1, 0:128], qq) * HALF_SCALE
                    t = jnp.tanh(half)
                    m = masks_t[d, r0:r1, c0:c1]
                    w = (half * (1.0 + t)).astype(BF16) * m
                    dw = dot_nt(kv[z, h, r0:r1, 128:256], gg)
                    ds = (dw * ((1.0 + t) * (1.0 + half * (1.0 - t)))).astype(BF16) * m
                    av, ak = dot_nn(w, gg), dot_nn(ds, qq)
                    if d == 0:
                        dv[h, r0:r1, :] = av
                        dk[h, r0:r1, :] = ak
                    else:
                        dv[h, r0:r1, :] += av
                        dk[h, r0:r1, :] += ak

    def pair_copy(b):
        return remote(s2.at[b], recv1.at[b], ss1.at[b], rs1.at[b], device(y, x, z, other))

    def weight(b, left, cols):
        @pl.loop(0, 4)
        def _(r):
            rows = pl.ds(pl.multiple_of(r * 256, 256), 256)
            tmp[...] = dot_tn(left[:, rows], cols).reshape(16, 2, 8, 512)
            half = pl.ds(pl.multiple_of(r * 128, 128), 128)
            part[b, half, :] = tmp[:, c].reshape(128, 512)
            s2[b, r] = tmp[:, other].reshape(4, 32, 512).astype(BF16)
        pair_copy(b).start()

    def plane_copies(b):
        out = []
        for d in (1, 2, 3):
            xx, yy = turn(x, d), turn(y, d)
            out.append(remote(s2.at[b, :, xx, :, pl.ds(0, 256)], r2a.at[b, d - 1], ss2.at[b, d - 1],
                              rs2.at[b, d - 1], device(y, xx, z, c)))
            out.append(remote(s2.at[b, yy, :, :, pl.ds(256, 256)], r2b.at[b, d - 1], ss2.at[b, d + 2],
                              rs2.at[b, d + 2], device(yy, x, z, c)))
        return out

    def line_copies(b):
        out = []
        for d in (1, 2, 3):
            xx, yy = turn(x, d), turn(y, d)
            out.append(remote(s3a.at[b, yy], r3a.at[b, d - 1], ss3.at[b, d - 1], rs3.at[b, d - 1],
                              device(yy, x, z, c)))
            out.append(remote(s3b.at[b, xx], r3b.at[b, d - 1], ss3.at[b, d + 2], rs3.at[b, d + 2],
                              device(y, xx, z, c)))
        return out

    def second(b):
        pair_copy(b).wait()
        for i in range(4):
            mine = part[b, i * 128:(i + 1) * 128, :].reshape(4, 32, 512)
            s2[b, i] = (mine + recv1[b, i].astype(F32)).astype(BF16)
        for cp in plane_copies(b):
            cp.start()

    def third(b):
        for cp in plane_copies(b):
            cp.wait()
        a = s2[b, :, x, :, 0:256].astype(F32)
        e = s2[b, y, :, :, 256:512].astype(F32)
        for d in range(3):
            a = a + r2a[b, d].astype(F32)
            e = e + r2b[b, d].astype(F32)
        s3a[b] = a.astype(BF16)
        s3b[b] = e.astype(BF16)
        for cp in line_copies(b):
            cp.start()

    def fourth(b):
        for cp in line_copies(b):
            cp.wait()
        a = s3a[b, y].astype(F32)
        e = s3b[b, x].astype(F32)
        for d in range(3):
            a = a + r3a[b, d].astype(F32)
            e = e + r3b[b, d].astype(F32)
        t4[:, :, b * 512:b * 512 + 256] = a.reshape(4, 8, 256)
        t4[:, :, b * 512 + 256:b * 512 + 512] = e.reshape(4, 8, 256)

    forward(0)
    for step in range(STEPS):
        before.arrive(step)
    queries.start()
    for d in range(1, 5):
        forward(d)

    @row_loop(256)
    def _(rows):
        a = jnp.concatenate([att[h, rows, :] for h in range(HEADS)], axis=1)
        no, inverse = stats(a)
        uu = u[rows, :].astype(F32)
        g = (no * uu).astype(BF16)
        gated[rows, :] = g
        output[rows, :] = (dot_nn(g, w_out[...]) + tokens[rows, :].astype(F32)).astype(BF16)
        gg = dot_nt(cot[rows, :], w_out[...])
        gh[rows, 0:512] = (gg * no * slope[rows, 0:512]).astype(BF16)
        gn = gg * uu
        back = inverse * (gn - jnp.mean(gn, axis=-1, keepdims=True)
                          - no * jnp.mean(gn * no, axis=-1, keepdims=True))
        back = back.astype(BF16)
        for h in range(HEADS):
            gs[mz, h, rows, :] = back[:, h * 128:(h + 1) * 128]

    grads.start()
    weight(0, cot, gated[...])
    weight(1, normed, gh[:, 0:512])
    query_back(0)
    for step in range(STEPS):
        queries.arrive(step)
    second(0)
    second(1)
    for d in range(1, 5):
        query_back(d)

    @row_loop(256)
    def _(rows):
        for h in range(HEADS):
            at = 1024 + h * 128
            gh[rows, at:at + 128] = (dq[h, rows, :] * HALF_SCALE * slope[rows, at:at + 128]).astype(BF16)

    weight(3, normed, gh[:, 1024:1536])
    key_back(0)
    second(3)
    for step in range(STEPS):
        grads.arrive(step)
    third(0)
    third(1)
    for d in range(1, 5):
        key_back(d)

    @row_loop(256)
    def _(rows):
        for h in range(HEADS):
            at = 512 + h * 128
            gh[rows, at:at + 128] = (dv[h, rows, :] * slope[rows, at:at + 128]).astype(BF16)
            at = 1536 + h * 128
            gh[rows, at:at + 128] = (dk[h, rows, :] * HALF_SCALE * slope[rows, at:at + 128]).astype(BF16)

    weight(2, normed, gh[:, 512:1024])
    weight(4, normed, gh[:, 1536:2048])
    third(3)
    second(2)
    second(4)

    @row_loop(256)
    def _(rows):
        up = dot_nt(gh[rows, :], w_in[...])
        zhat, inverse = stats(tokens[rows, :].astype(F32))
        back = inverse * (up - jnp.mean(up, axis=-1, keepdims=True)
                          - zhat * jnp.mean(up * zhat, axis=-1, keepdims=True))
        grad_tokens[rows, :] = (back + cot[rows, :].astype(F32)).astype(BF16)

    fourth(0)
    fourth(1)
    fourth(3)
    third(2)
    third(4)
    fourth(2)
    fourth(4)
    last = []
    for d in (1, 2, 3):
        zz = turn(z, d)
        cp = remote(t4.at[zz], r4.at[d - 1], ss4.at[d - 1], rs4.at[d - 1], device(y, x, zz, c))
        cp.start()
        last.append(cp)
    before.drain()
    queries.drain()
    grads.drain()
    for cp in last:
        cp.wait()
    total = t4[z] + r4[0] + r4[1] + r4[2]
    out_out[...] = total[:, 0:512]
    out_in[...] = total[:, 512:2560]


def local(tokens_in, user_ids, w_in, w_out, cotangent):
    vmem = pl.BlockSpec(memory_space=pltpu.VMEM)
    dma = pltpu.SemaphoreType.DMA

    def gather_sems():
        return [dma((4, 4, 2)), dma((4, 4)), dma((4, 4)), dma((4, 4))]

    output, grad_tokens, total_in, total_out = pl.pallas_call(
        layer_kernel,
        name="layer",
        out_shape=(
            jax.ShapeDtypeStruct((ROWS, 1024), BF16),
            jax.ShapeDtypeStruct((ROWS, 1024), BF16),
            jax.ShapeDtypeStruct((8, 2048), F32),
            jax.ShapeDtypeStruct((8, 512), F32),
        ),
        in_specs=[vmem] * 5,
        out_specs=(vmem,) * 4,
        scratch_shapes=[
            pltpu.VMEM((ROWS, 1024), BF16),
            pltpu.VMEM((ROWS, 2048), F32),
            pltpu.VMEM((ROWS, 512), BF16),
            pltpu.VMEM((4, 4, ROWS, 256), BF16),
            pltpu.VMEM((4, 4, ROWS, 256), BF16),
            pltpu.VMEM((4, 4, ROWS, 128), BF16),
            pltpu.VMEM((4, 4, ROWS, 128), BF16),
            pltpu.VMEM((4, 4, ROWS, 128), BF16),
            pltpu.VMEM((4, 4, ROWS, 128), BF16),
            pltpu.VMEM((4, ROWS, 128), F32),
            pltpu.VMEM((4, ROWS, 128), F32),
            pltpu.VMEM((4, ROWS, 128), F32),
            pltpu.VMEM((4, ROWS, 128), F32),
            pltpu.VMEM((ROWS, 512), BF16),
            pltpu.VMEM((ROWS, 2048), BF16),
            pltpu.VMEM((5, ROWS, ROWS), BF16),
            pltpu.VMEM((5, ROWS, ROWS), BF16),
            pltpu.VMEM((16, 2, 8, 512), F32),
            pltpu.VMEM((NB, 512, 512), F32),
            pltpu.VMEM((NB, 4, 4, 32, 512), BF16),
            pltpu.VMEM((NB, 4, 4, 32, 512), BF16),
            pltpu.VMEM((NB, 3, 4, 32, 256), BF16),
            pltpu.VMEM((NB, 3, 4, 32, 256), BF16),
            pltpu.VMEM((NB, 4, 32, 256), BF16),
            pltpu.VMEM((NB, 4, 32, 256), BF16),
            pltpu.VMEM((NB, 3, 32, 256), BF16),
            pltpu.VMEM((NB, 3, 32, 256), BF16),
            pltpu.VMEM((4, 8, NB * 512), F32),
            pltpu.VMEM((3, 8, NB * 512), F32),
            *gather_sems(), *gather_sems(), *gather_sems(),
            dma((NB,)), dma((NB,)), dma((NB, 6)), dma((NB, 6)), dma((NB, 6)), dma((NB, 6)),
            dma((3,)), dma((3,)),
        ],
        compiler_params=pltpu.CompilerParams(
            collective_id=0, has_side_effects=True, vmem_limit_bytes=67043328),
    )(tokens_in[0], user_ids, w_in, w_out, cotangent[0])
    return output[None], grad_tokens[None], total_in, total_out.T


def solution(mesh):
    in_specs = (P("dp", "seq", None), P("dp", None), P(), P(), P("dp", "seq", None))
    out_specs = (
        P("dp", "seq", None),
        P("dp", "seq", None),
        P(("dp", "seq"), None),
        P(None, ("dp", "seq")),
    )
    return jax.shard_map(local, mesh=mesh, in_specs=in_specs, out_specs=out_specs, check_vma=False)
```

time: 1490 us -> 135 us (0.09)
  waiting for transfers between devices: 1270 us -> 0 us
  Pallas kernels: 0 us -> 128 us
  matrix products: 93.9 us -> 0 us
  starting transfers between devices: 42.8 us -> 0 us
  local copies, waits for them, and re-layouts: 40 us -> 5.8 us
  other arithmetic: 17.2 us -> 0 us
    reduce_scatter x2 -> x0, waiting for transfers between devices: 1240 us -> none  [the longest x1 654 us: local(): lax.psum_scatter(grad_w_in, ('dp', 'seq'), scatter_dimension=0, tiled=True)]
    pallas_call x0 -> x1, Pallas kernels: none -> 128 us  [local(): pl.pallas_call(layer_kernel, name='layer', out_shape=(jax.ShapeDtypeStruc...]
    dot_general x36 -> x0, matrix products: 93.9 us -> none  [the longest x5 19.2 us: local(): jnp.einsum('qhd,khd->hqk', query_heads, key_heads, preferred_element_type...]
    ppermute x16 -> x0, starting transfers between devices: 42.4 us -> none  [from_behind(): return lax.ppermute(value, axis, pairs)]
    ppermute x16 -> x0, waiting for transfers between devices: 31 us -> none  [from_behind(): return lax.ppermute(value, axis, pairs)]
    reshape x10 -> x0, local copies, waits for them, and re-layouts: 16.2 us -> none  [the longest x5 9.46 us: local(): key_heads = piece_keys.reshape(n_rows, HEADS, HD)]
    convert_element_type x8 -> x0, local copies, waits for them, and re-layouts: 15.6 us -> none  [the longest x4 8.31 us: local(): key_terms[distance][0].astype(jnp.bfloat16)]
  transfers between devices with their start and end apart: 18 -> 0, of which waited for: 8 -> 0; matrix products, arithmetic and copies ran while one was open for 6% -> 0% of each run, Pallas kernels for 0% -> 0%
where the time goes in v1:
time: 135 us
  Pallas kernels  128 us (95%)
  local copies, waits for them, and re-layouts  5.8 us (4%)
    pallas_call x1, Pallas kernels, local(): pl.pallas_call(layer_kernel, name='layer', out_shape=(jax.ShapeDtypeStruc...  128 us
    unnamed x8, local copies, waits for them, and re-layouts  5.8 us

profile of v1, /device:TPU:0, one launch (start us, length us, event | category | flops | bytes accessed | tf_op | source)
XLA Modules:
  0.0 134.9 jit_solution(8610898398230780475)
XLA Ops:
  0.6 128.4 %layer.1 = (bf16[512,1024]{1,0:T(8,128)(2,1)}, bf16[512,1024]{1,0:T(8,128)(2,1)}, f32[8,2048]{1,0:T(8,128)}, f32[8,512]{1,0:T(8,128)}) custom-call(bf16[512,1024]{1,0:T(8,128)(2,1)} %bitcast.5, s32[1,4096]{1,0:T(1,128)} %ids.1, bf16[1024,2048]{1,0:T(8,128)(2,1)} %w_in.1, bf16[512,1024]{1,0:T(8,128)(2,1)} %w_out.1, bf16[512,1024]{1,0:T(8,128)(2,1)} %bitcast.6), custom_call_target="tpu_custom_call" | custom-call | tf_op jit(solution)/shard_map/layer/pallas_call | solution.py:482
  129.1 0.0 copy-start
  129.1 0.0 copy-start.1
  129.1 2.3 %copy.13 = bf16[1,512,1024]{2,1,0:T(8,128)(2,1)} copy(bf16[1,512,1024]{2,1,0:T(8,128)(2,1)} %bitcast.8) | data formatting | bytes 2097152
  131.4 2.3 %copy.14 = bf16[1,512,1024]{2,1,0:T(8,128)(2,1)} copy(bf16[1,512,1024]{2,1,0:T(8,128)(2,1)} %bitcast.7) | data formatting | bytes 2097152
  133.6 0.0 copy-done
  133.6 0.6 copy.15
  134.3 0.0 copy-done.1
  134.3 0.6 copy.16
Async XLA Ops:
  129.1 4.6 %copy-start = (f32[8,2048]{1,0:T(8,128)S(1)}, f32[8,2048]{1,0:T(8,128)}, u32[]{:S(2)}) copy-start(f32[8,2048]{1,0:T(8,128)} %get-tuple-element.18) | copy-start | bytes 196612
  129.1 5.2 %copy-start.1 = (f32[8,512]{1,0:T(8,128)S(1)}, f32[8,512]{1,0:T(8,128)}, u32[]{:S(2)}) copy-start(f32[8,512]{1,0:T(8,128)} %get-tuple-element.11) | copy-start | bytes 49156

commit v2 on v1

--- a/solution.py
+++ b/solution.py
@@ -37,6 +37,32 @@
     3: ((2, 0), (0, 2), (2, 1), (0, 3), (2, 2), (1, 3), (2, 3), (1, 1), (1, 2), (1, 0)),
 }
 STEPS = 10
+QUERY_MOVES = (
+    (0, 1, 0, (0, 1)),
+    (0, 3, 0, (2, 3)),
+    (1, 2, 1, (0, 1, 2, 3)),
+    (2, 3, 2, (0, 1, 2, 3)),
+    (1, 0, 1, (3, 2)),
+    (0, 1, 0, (2, 3)),
+)
+QUERY_RELAYS = {
+    (1, 0, 0): 2, (1, 0, 1): 2,
+    (3, 0, 2): 2, (3, 0, 3): 2,
+    (2, 1, 0): 3, (2, 1, 1): 3,
+    (0, 1, 3): 3, (0, 1, 2): 3,
+}
+QUERY_ARRIVALS = {
+    0: ((1, 3), (1, 2)),
+    1: ((0, 0), (0, 1), (0, 2), (0, 3)),
+    2: ((1, 0), (1, 1), (1, 2), (1, 3), (0, 2), (0, 3), (0, 0), (0, 1)),
+    3: ((0, 2), (0, 3), (2, 0), (2, 1), (2, 2), (2, 3), (1, 0), (1, 1), (1, 3), (1, 2)),
+}
+GRAD_ARRIVALS = {
+    0: ((1, 3), (1, 1), (1, 2)),
+    1: ((0, 0), (0, 1), (0, 2), (0, 3)),
+    2: ((1, 0), (1, 1), (0, 2), (1, 2), (0, 0), (0, 3), (0, 1), (1, 3)),
+    3: ((2, 0), (2, 1), (0, 2), (2, 2), (0, 3), (2, 3), (1, 3), (1, 1), (1, 0), (1, 2)),
+}
 
 
 def place():
@@ -71,10 +97,11 @@
 
 
 class Gather:
-    def __init__(self, near, far, sems, chip, core, target):
-        self.near, self.far = near, far
+    def __init__(self, buf, sems, chip, core, target, moves, relays, arrivals):
+        self.buf, self.near, self.far = buf, buf.at[0], buf.at[1]
         self.ss, self.rs, self.sp, self.rp = sems
         self.chip, self.core, self.target = chip, core, target
+        self.moves, self.relays, self.arrivals = moves, relays, arrivals
 
     def move(self, sender, receiver, owner, h):
         k = 0 if receiver == sender + 1 else 1
@@ -85,19 +112,21 @@
         return remote(self.near.at[owner, h], self.far.at[owner, h], self.sp.at[owner, h],
                       self.rp.at[owner, h], self.target(self.chip, 1 - self.core))
 
-    def start(self):
-        @pl.when(self.core == 0)
-        def _():
-            for h in range(HEADS):
-                self.share(self.chip, h).start()
-        for sender, receiver, owner, heads in OWN_MOVES:
+    def start(self, moves=None, share=True):
+        if share:
+            @pl.when(self.core == 0)
+            def _():
+                for h in range(HEADS):
+                    self.share(self.chip, h).start()
+        for sender, receiver, owner, heads in (self.moves if moves is None else moves):
             @pl.when(self.chip == sender)
             def _():
                 for h in heads:
                     self.move(sender, receiver, owner, h).start()
 
-    def arrive(self, step):
-        for role, order in ARRIVALS.items():
+    def arrive(self, step, roles=(0, 1, 2, 3)):
+        for role in roles:
+            order = self.arrivals.get(role, ())
             if step >= len(order):
                 continue
             owner, h = order[step]
@@ -105,8 +134,8 @@
             @pl.when(self.chip == role)
             def _():
                 self.move(role, (role + 1) % 4, owner, h).wait_recv()
-                if (role, owner, h) in RELAYS:
-                    self.move(role, RELAYS[role, owner, h], owner, h).start()
+                if (role, owner, h) in self.relays:
+                    self.move(role, self.relays[role, owner, h], owner, h).start()
                 if owner == role - 1:
                     self.share(owner, h).start()
                 if owner == role - 2:
@@ -114,21 +143,51 @@
                     def _():
                         self.share(owner, h).start()
 
+    def look(self, step):
+        code = jnp.int32(-1)
+        for role, order in self.arrivals.items():
+            for k, (owner, h) in enumerate(order):
+                value = (self.relays.get((role, owner, h), -1) + 1) * 16 + owner * 4 + h
+                code = jnp.where((self.chip == role) & (step == k), value, code)
+        return code >= 0, (code // 4) % 4, code % 4, code // 16 - 1
+
+    def service(self, step, serve=None):
+        wanted, owner, h, dest = self.look(step)
+        if serve is not None:
+            wanted = wanted & serve
+
+        @pl.when(wanted)
+        def _():
+            here = self.near.at[owner, h]
+            gap = self.chip - owner
+            remote(here, here, self.ss.at[owner, h, 0], self.rs.at[owner, h],
+                   self.target(turn(self.chip, 1), self.core)).wait_recv()
+
+            @pl.when(dest >= 0)
+            def _():
+                k = jnp.where(dest == self.chip + 1, 0, 1)
+                remote(here, here, self.ss.at[owner, h, k], self.rs.at[owner, h],
+                       self.target(dest, self.core)).start()
+
+            @pl.when((gap == 1) | ((gap == 2) & (self.core == 1)))
+            def _():
+                self.share(owner, h).start()
+
     def drain(self):
         @pl.when(self.core == 0)
         def _():
             for h in range(HEADS):
                 self.share(self.chip, h).wait_send()
-        for sender, receiver, owner, heads in OWN_MOVES:
+        for sender, receiver, owner, heads in self.moves:
             @pl.when(self.chip == sender)
             def _():
                 for h in heads:
                     self.move(sender, receiver, owner, h).wait_send()
-        for (role, owner, h), receiver in RELAYS.items():
+        for (role, owner, h), receiver in self.relays.items():
             @pl.when(self.chip == role)
             def _():
                 self.move(role, receiver, owner, h).wait_send()
-        for role, order in ARRIVALS.items():
+        for role, order in self.arrivals.items():
             for owner, h in order:
                 if owner == role - 1:
                     @pl.when(self.chip == role)
@@ -139,21 +198,9 @@
                     def _():
                         self.share(owner, h).wait_send()
 
-    def block(self, d):
-        if d == 0:
-            return self.near, self.chip
-        if d % 2 == 0:
-            return self.near, self.chip - d // 2
-        return self.far, self.chip - (d + 1) // 2 + self.core
-
-    def wait_share(self, d, h):
-        if d % 2 == 1:
-            owner = self.chip - (d + 1) // 2 + self.core
-            self.share(owner, h).wait_recv()
-
-
-def layer_kernel(tokens, ids, w_in, w_out, cot, output, grad_tokens, out_in, out_out,
-                 normed, slope, u, kv, kv2, qs, qs2, gs, gs2, att, dq, dk, dv, gated, gh, masks, masks_t,
+
+def layer_kernel(tokens_hbm, ids, w_in_hbm, w_out_hbm, cot_hbm, output_hbm, grad_tokens_hbm, out_in, out_out,
+                 output, grad_tokens, out_sems, tokens, w_in, w_out, cot, in_sems, normed_t, cot_t, normed, slope, u, kv, qs, gs, att, dq, dk, dv, gated, gh, masks, masks_t,
                  tmp, part, s2, recv1, r2a, r2b, s3a, s3b, r3a, r3b, t4, r4,
                  kss, krs, ksp, krp, qss, qrs, qsp, qrp, gss, grs, gsp, grp,
                  ss1, rs1, ss2, rs2, ss3, rs3, ss4, rs4):
@@ -168,14 +215,28 @@
     for t in peers:
         pl.semaphore_signal(barrier, inc=1, device_id=t, device_id_type=MESH)
 
-    before = Gather(kv, kv2, (kss, krs, ksp, krp), z, c, lambda zz, cc: device(y, x, zz, cc))
+    tokens_in = pltpu.make_async_copy(tokens_hbm, tokens, in_sems.at[0])
+    tokens_in.start()
+    w_ins = {}
+    for i, col in enumerate((1536, 512, 1024, 0)):
+        cols = pl.ds(col, 512)
+        w_ins[col] = pltpu.make_async_copy(w_in_hbm.at[:, cols], w_in.at[:, cols], in_sems.at[1 + i])
+        w_ins[col].start()
+    cot_in = pltpu.make_async_copy(cot_hbm, cot, in_sems.at[5])
+    w_out_in = pltpu.make_async_copy(w_out_hbm, w_out, in_sems.at[6])
+    cot_in.start()
+    w_out_in.start()
     mz, mc = 3 - z, 1 - c
 
     def mirrored(zz, cc):
         return device(y, x, 3 - zz, 1 - cc)
 
-    queries = Gather(qs, qs2, (qss, qrs, qsp, qrp), mz, mc, mirrored)
-    grads = Gather(gs, gs2, (gss, grs, gsp, grp), mz, mc, mirrored)
+    before = Gather(kv, (kss, krs, ksp, krp), z, c, lambda zz, cc: device(y, x, zz, cc),
+                    OWN_MOVES, RELAYS, ARRIVALS)
+    queries = Gather(qs, (qss, qrs, qsp, qrp), mz, mc, mirrored,
+                     QUERY_MOVES, QUERY_RELAYS, QUERY_ARRIVALS)
+    grads = Gather(gs, (gss, grs, gsp, grp), mz, mc, mirrored,
+                   OWN_MOVES, RELAYS, GRAD_ARRIVALS)
 
     def stats(v):
         center = v - jnp.mean(v, axis=-1, keepdims=True)
@@ -189,11 +250,15 @@
                 body(pl.ds(pl.multiple_of(i * size, size), size))
         return wrap
 
+    tokens_in.wait()
+
     @row_loop(128)
     def _(rows):
         normed[rows, :] = stats(tokens[rows, :].astype(F32))[0].astype(BF16)
 
     def features(col, put):
+        w_ins[col].wait()
+
         @row_loop(256)
         def _(rows):
             half = 0.5 * dot_nn(normed[rows, :], w_in[:, col:col + 512])
@@ -203,15 +268,15 @@
 
     def put_k(rows, a):
         for h in range(HEADS):
-            kv[z, h, rows, 0:128] = a[:, h * 128:(h + 1) * 128]
+            kv[0, z, h, rows, 0:128] = a[:, h * 128:(h + 1) * 128]
 
     def put_v(rows, a):
         for h in range(HEADS):
-            kv[z, h, rows, 128:256] = a[:, h * 128:(h + 1) * 128]
+            kv[0, z, h, rows, 128:256] = a[:, h * 128:(h + 1) * 128]
 
     def put_q(rows, a):
         for h in range(HEADS):
-            qs[mz, h, rows, :] = a[:, h * 128:(h + 1) * 128]
+            qs[0, mz, h, rows, :] = a[:, h * 128:(h + 1) * 128]
 
     def put_u(rows, a):
         u[rows, :] = a
@@ -221,6 +286,7 @@
     pl.semaphore_wait(barrier, len(peers))
     before.start()
     features(1024, put_q)
+    queries.start(QUERY_MOVES[:4])
     features(0, put_u)
 
     def ids_of(b):
@@ -241,75 +307,123 @@
         masks[d] = jnp.where(same, one, nil).astype(BF16)
         masks_t[d] = jnp.where(same_t, one, nil).astype(BF16)
 
-    def spans(d, flip):
-        if d == 0:
-            pair = ((0, 256), (0, 512)) if not flip else ((0, 512), (256, 512))
-        elif d == 4:
-            pair = ((0, 512), (256, 512)) if not flip else ((0, 256), (0, 512))
-        else:
-            pair = ((0, 512), (0, 512))
-        return ((0, 256) + pair[0], (256, 512) + pair[1])
-
-    def forward(d):
-        @pl.when(block >= d)
+    def pipeline(items, scores, weigh, add):
+        ahead = scores(*items[0])
+        for i, item in enumerate(items):
+            now = ahead
+            if i + 1 < len(items):
+                ahead = scores(*items[i + 1])
+            add(item, weigh(now, item))
+
+    def tiles(where, flip, heads, d):
+        out = []
+        for h in heads:
+            for r in (0, 256):
+                cols = (0, 512)
+                if isinstance(d, int) and d == 0:
+                    cols = ((0, 256), (0, 512))[r // 256] if not flip else ((0, 512), (256, 512))[r // 256]
+                out.append(where + (h, d, (r, r + 256), cols))
+        return out
+
+    def forward_tiles(items, first=False):
+        def scores(e, o, h, d, rows, cols):
+            return dot_nt(qs[0, mz, h, rows[0]:rows[1], :], kv[e, o, h, cols[0]:cols[1], 0:128])
+
+        def weigh(now, item):
+            e, o, h, d, rows, cols = item
+            half = (now * HALF_SCALE).astype(BF16)
+            return (half + half * jnp.tanh(half)) * masks[d, rows[0]:rows[1], cols[0]:cols[1]]
+
+        def add(item, w):
+            e, o, h, d, rows, cols = item
+            a = dot_nn(w, kv[e, o, h, cols[0]:cols[1], 128:256])
+            if first:
+                att[h, rows[0]:rows[1], :] = a
+            else:
+                att[h, rows[0]:rows[1], :] += a
+
+        pipeline(items, scores, weigh, add)
+
+    def query_tiles(items, first=False):
+        def scores(e, o, h, d, rows, cols):
+            keys = slice(cols[0], cols[1])
+            mine = slice(rows[0], rows[1])
+            return (dot_nt(qs[0, mz, h, mine, :], kv[e, o, h, keys, 0:128]),
+                    dot_nt(gs[0, mz, h, mine, :], kv[e, o, h, keys, 128:256]))
+
+        def weigh(now, item):
+            e, o, h, d, rows, cols = item
+            half = (now[0] * HALF_SCALE).astype(BF16)
+            t = jnp.tanh(half)
+            a = (t + 1) * masks[d, rows[0]:rows[1], cols[0]:cols[1]]
+            return now[1].astype(BF16) * (a + half * a * (1 - t))
+
+        def add(item, ds):
+            e, o, h, d, rows, cols = item
+            a = dot_nn(ds, kv[e, o, h, cols[0]:cols[1], 0:128])
+            if first:
+                dq[h, rows[0]:rows[1], :] = a
+            else:
+                dq[h, rows[0]:rows[1], :] += a
+
+        pipeline(items, scores, weigh, add)
+
+    def key_tiles(items, first=False):
+        def scores(e, o, h, d, rows, cols):
+            theirs = slice(cols[0], cols[1])
+            mine = slice(rows[0], rows[1])
+            return (dot_nt(kv[0, z, h, mine, 0:128], qs[e, o, h, theirs, :]),
+                    dot_nt(kv[0, z, h, mine, 128:256], gs[e, o, h, theirs, :]))
+
+        def weigh(now, item):
+            e, o, h, d, rows, cols = item
+            half = (now[0] * HALF_SCALE).astype(BF16)
+            t = jnp.tanh(half)
+            a = (t + 1) * masks_t[d, rows[0]:rows[1], cols[0]:cols[1]]
+            w = half * a
+            return w, now[1].astype(BF16) * (a + w * (1 - t))
+
+        def add(item, got):
+            e, o, h, d, rows, cols = item
+            av = dot_nn(got[0], gs[e, o, h, cols[0]:cols[1], :])
+            ak = dot_nn(got[1], qs[e, o, h, cols[0]:cols[1], :])
+            if first:
+                dv[h, rows[0]:rows[1], :] = av
+                dk[h, rows[0]:rows[1], :] = ak
+            else:
+                dv[h, rows[0]:rows[1], :] += av
+                dk[h, rows[0]:rows[1], :] += ak
+
+        pipeline(items, scores, weigh, add)
+
+    def meet(gather, step, compute, flip, also=None):
+        there, o, h, _ = gather.look(step)
+        gap = gather.chip - o
+        even = 2 * gap
+        odd = even + 2 * gather.core - 1
+
+        @pl.when(there & ((gap == 1) | ((gap == 2) & (gather.core == 0))))
         def _():
-            ref, i = before.block(d)
-
-            @pl.loop(0, HEADS)
-            def _(h):
-                before.wait_share(d, h)
-                for r0, r1, c0, c1 in spans(d, False):
-                    half = dot_nt(qs[mz, h, r0:r1, :], ref[i, h, c0:c1, 0:128]) * HALF_SCALE
-                    w = (half * (1.0 + jnp.tanh(half))).astype(BF16) * masks[d, r0:r1, c0:c1]
-                    a = dot_nn(w, ref[i, h, c0:c1, 128:256])
-                    if d == 0:
-                        att[h, r0:r1, :] = a
-                    else:
-                        att[h, r0:r1, :] += a
-
-    def query_back(d):
-        @pl.when(block >= d)
+            gather.share(o, h).wait_recv()
+            if also is not None:
+                also.share(o, h).wait_recv()
+            compute(tiles((0, o), flip, (h,), even) + tiles((1, o), flip, (h,), odd))
+
+        @pl.when(there & (gap == 2) & (gather.core == 1))
         def _():
-            ref, i = before.block(d)
-
-            @pl.loop(0, HEADS)
-            def _(h):
-                for r0, r1, c0, c1 in spans(d, False):
-                    half = dot_nt(qs[mz, h, r0:r1, :], ref[i, h, c0:c1, 0:128]) * HALF_SCALE
-                    t = jnp.tanh(half)
-                    dw = dot_nt(gs[mz, h, r0:r1, :], ref[i, h, c0:c1, 128:256])
-                    ds = (dw * ((1.0 + t) * (1.0 + half * (1.0 - t)))).astype(BF16) * masks[d, r0:r1, c0:c1]
-                    a = dot_nn(ds, ref[i, h, c0:c1, 0:128])
-                    if d == 0:
-                        dq[h, r0:r1, :] = a
-                    else:
-                        dq[h, r0:r1, :] += a
-
-    def key_back(d):
-        @pl.when(block + d <= 7)
+            compute(tiles((0, o), flip, (h,), even))
+
+    def beside(gather, compute, flip, also=None):
+        @pl.when(gather.core == 1)
         def _():
-            qref, i = queries.block(d)
-            gref, _ = grads.block(d)
-
-            @pl.loop(0, HEADS)
-            def _(h):
-                queries.wait_share(d, h)
-                grads.wait_share(d, h)
-                for r0, r1, c0, c1 in spans(d, True):
-                    qq, gg = qref[i, h, c0:c1, :], gref[i, h, c0:c1, :]
-                    half = dot_nt(kv[z, h, r0:r1, 0:128], qq) * HALF_SCALE
-                    t = jnp.tanh(half)
-                    m = masks_t[d, r0:r1, c0:c1]
-                    w = (half * (1.0 + t)).astype(BF16) * m
-                    dw = dot_nt(kv[z, h, r0:r1, 128:256], gg)
-                    ds = (dw * ((1.0 + t) * (1.0 + half * (1.0 - t)))).astype(BF16) * m
-                    av, ak = dot_nn(w, gg), dot_nn(ds, qq)
-                    if d == 0:
-                        dv[h, r0:r1, :] = av
-                        dk[h, r0:r1, :] = ak
-                    else:
-                        dv[h, r0:r1, :] += av
-                        dk[h, r0:r1, :] += ak
+            @pl.loop(0, 2)
+            def _(pair):
+                heads = (2 * pair, 2 * pair + 1)
+                for h in heads:
+                    gather.share(gather.chip, h).wait_recv()
+                    if also is not None:
+                        also.share(gather.chip, h).wait_recv()
+                compute(tiles((1, gather.chip), flip, heads, 1))
 
     def pair_copy(b):
         return remote(s2.at[b], recv1.at[b], ss1.at[b], rs1.at[b], device(y, x, z, other))
@@ -318,7 +432,7 @@
         @pl.loop(0, 4)
         def _(r):
             rows = pl.ds(pl.multiple_of(r * 256, 256), 256)
-            tmp[...] = dot_tn(left[:, rows], cols).reshape(16, 2, 8, 512)
+            tmp[...] = dot_nn(left[rows, :], cols).reshape(16, 2, 8, 512)
             half = pl.ds(pl.multiple_of(r * 128, 128), 128)
             part[b, half, :] = tmp[:, c].reshape(128, 512)
             s2[b, r] = tmp[:, other].reshape(4, 32, 512).astype(BF16)
@@ -376,12 +490,31 @@
         t4[:, :, b * 512:b * 512 + 256] = a.reshape(4, 8, 256)
         t4[:, :, b * 512 + 256:b * 512 + 512] = e.reshape(4, 8, 256)
 
-    forward(0)
-    for step in range(STEPS):
-        before.arrive(step)
-    queries.start()
-    for d in range(1, 5):
-        forward(d)
+    forward_tiles(tiles((0, z), False, range(HEADS), 0), first=True)
+    cot_in.wait()
+    w_out_in.wait()
+
+    @row_loop(128)
+    def _(rows):
+        normed_t[:, rows] = jnp.transpose(normed[rows, :])
+        cot_t[:, rows] = jnp.transpose(cot[rows, :])
+
+    beside(before, forward_tiles, False)
+    before.service(0)
+    before.service(1)
+    queries.start(QUERY_MOVES[4:5], share=False)
+    for step in range(2):
+        queries.arrive(step, roles=(1, 2, 3))
+
+    @pl.loop(0, STEPS)
+    def _(step):
+        meet(before, step, forward_tiles, False)
+        before.service(step + 2)
+
+        @pl.when(step == 3)
+        def _():
+            queries.start(QUERY_MOVES[5:], share=False)
+
 
     @row_loop(256)
     def _(rows):
@@ -398,18 +531,31 @@
                           - no * jnp.mean(gn * no, axis=-1, keepdims=True))
         back = back.astype(BF16)
         for h in range(HEADS):
-            gs[mz, h, rows, :] = back[:, h * 128:(h + 1) * 128]
+            gs[0, mz, h, rows, :] = back[:, h * 128:(h + 1) * 128]
 
     grads.start()
-    weight(0, cot, gated[...])
-    weight(1, normed, gh[:, 0:512])
-    query_back(0)
-    for step in range(STEPS):
-        queries.arrive(step)
+    output_out = pltpu.make_async_copy(output, output_hbm, out_sems.at[0])
+    output_out.start()
+    query_tiles(tiles((0, z), False, range(HEADS), 0), first=True)
+    weight(0, cot_t, gated[...])
+    weight(1, normed_t, gh[:, 0:512])
+    queries.arrive(0, roles=(0,))
+    queries.arrive(1, roles=(0,))
+    queries.arrive(2, roles=(1,))
+    early = mz < 2
+
+    @pl.loop(1, 5)
+    def _(d):
+        grads.service(d - 1, serve=early)
+
+        @pl.when(block >= d)
+        def _():
+            owner = jnp.where(d % 2 == 0, z - d // 2, z - (d + 1) // 2 + c)
+            query_tiles(tiles((d % 2, owner), False, range(HEADS), d))
+
     second(0)
     second(1)
-    for d in range(1, 5):
-        query_back(d)
+    queries.arrive(3, roles=(1,))
 
     @row_loop(256)
     def _(rows):
@@ -417,15 +563,23 @@
             at = 1024 + h * 128
             gh[rows, at:at + 128] = (dq[h, rows, :] * HALF_SCALE * slope[rows, at:at + 128]).astype(BF16)
 
-    weight(3, normed, gh[:, 1024:1536])
-    key_back(0)
+    weight(3, normed_t, gh[:, 1024:1536])
+    key_tiles(tiles((0, mz), True, range(HEADS), 0), first=True)
+    beside(grads, key_tiles, True, also=queries)
     second(3)
-    for step in range(STEPS):
-        grads.arrive(step)
     third(0)
     third(1)
-    for d in range(1, 5):
-        key_back(d)
+    late = mz >= 2
+    grads.service(0, serve=late)
+    for step in range(2, 8):
+        queries.arrive(step, roles=(2,))
+    for step in range(2, STEPS):
+        queries.arrive(step, roles=(3,))
+
+    @pl.loop(0, STEPS)
+    def _(step):
+        grads.service(step + 1, serve=late)
+        meet(grads, step, key_tiles, True, also=queries)
 
     @row_loop(256)
     def _(rows):
@@ -435,8 +589,8 @@
             at = 1536 + h * 128
             gh[rows, at:at + 128] = (dk[h, rows, :] * HALF_SCALE * slope[rows, at:at + 128]).astype(BF16)
 
-    weight(2, normed, gh[:, 512:1024])
-    weight(4, normed, gh[:, 1536:2048])
+    weight(2, normed_t, gh[:, 512:1024])
+    weight(4, normed_t, gh[:, 1536:2048])
     third(3)
     second(2)
     second(4)
@@ -449,6 +603,8 @@
                           - zhat * jnp.mean(up * zhat, axis=-1, keepdims=True))
         grad_tokens[rows, :] = (back + cot[rows, :].astype(F32)).astype(BF16)
 
+    tokens_out = pltpu.make_async_copy(grad_tokens, grad_tokens_hbm, out_sems.at[1])
+    tokens_out.start()
     fourth(0)
     fourth(1)
     fourth(3)
@@ -465,6 +621,8 @@
     before.drain()
     queries.drain()
     grads.drain()
+    output_out.wait()
+    tokens_out.wait()
     for cp in last:
         cp.wait()
     total = t4[z] + r4[0] + r4[1] + r4[2]
@@ -472,8 +630,56 @@
     out_in[...] = total[:, 512:2560]
 
 
+def finish_kernel(a, b, p, q, out_a, out_b, out_p, out_q, va, vb, vp, vq, ins, outs):
+    moves = []
+    for i in range(4):
+        rows = pl.ds(i * 128, 128)
+        moves.append((a.at[rows, :], va.at[rows, :], out_a.at[0, rows, :]))
+        moves.append((b.at[rows, :], vb.at[rows, :], out_b.at[0, rows, :]))
+    moves.append((p, vp, out_p))
+    fetch = [pltpu.make_async_copy(q, vq, ins.at[9])]
+    fetch += [pltpu.make_async_copy(src, mid, ins.at[i]) for i, (src, mid, _) in enumerate(moves)]
+    store = [pltpu.make_async_copy(mid, dst, outs.at[i]) for i, (_, mid, dst) in enumerate(moves)]
+    last = pltpu.make_async_copy(vq, out_q, outs.at[9])
+    for cp in fetch:
+        cp.start()
+    fetch[0].wait()
+    last.start()
+    for got, put in zip(fetch[1:], store):
+        got.wait()
+        put.start()
+    for put in store:
+        put.wait()
+    last.wait()
+
+
+def finish(output, grad_tokens, total_in, total_out):
+    hbm = pl.BlockSpec(memory_space=pl.ANY)
+    dma = pltpu.SemaphoreType.DMA
+    return pl.pallas_call(
+        finish_kernel,
+        name="finish",
+        out_shape=(
+            jax.ShapeDtypeStruct((1, ROWS, 1024), BF16),
+            jax.ShapeDtypeStruct((1, ROWS, 1024), BF16),
+            jax.ShapeDtypeStruct((8, 2048), F32),
+            jax.ShapeDtypeStruct((8, 512), F32),
+        ),
+        in_specs=[hbm] * 4,
+        out_specs=(hbm,) * 4,
+        scratch_shapes=[
+            pltpu.VMEM((ROWS, 1024), BF16),
+            pltpu.VMEM((ROWS, 1024), BF16),
+            pltpu.VMEM((8, 2048), F32),
+            pltpu.VMEM((8, 512), F32),
+            dma((10,)), dma((10,)),
+        ],
+    )(output, grad_tokens, total_in, total_out)
+
+
 def local(tokens_in, user_ids, w_in, w_out, cotangent):
     vmem = pl.BlockSpec(memory_space=pltpu.VMEM)
+    hbm = pl.BlockSpec(memory_space=pl.ANY)
     dma = pltpu.SemaphoreType.DMA
 
     def gather_sems():
@@ -488,18 +694,25 @@
             jax.ShapeDtypeStruct((8, 2048), F32),
             jax.ShapeDtypeStruct((8, 512), F32),
         ),
-        in_specs=[vmem] * 5,
-        out_specs=(vmem,) * 4,
+        in_specs=[hbm, vmem, hbm, hbm, hbm],
+        out_specs=(hbm, hbm, vmem, vmem),
         scratch_shapes=[
+            pltpu.VMEM((ROWS, 1024), BF16),
+            pltpu.VMEM((ROWS, 1024), BF16),
+            dma((2,)),
+            pltpu.VMEM((ROWS, 1024), BF16),
+            pltpu.VMEM((1024, 2048), BF16),
+            pltpu.VMEM((512, 1024), BF16),
+            pltpu.VMEM((ROWS, 1024), BF16),
+            dma((7,)),
+            pltpu.VMEM((1024, ROWS), BF16),
+            pltpu.VMEM((1024, ROWS), BF16),
             pltpu.VMEM((ROWS, 1024), BF16),
             pltpu.VMEM((ROWS, 2048), F32),
             pltpu.VMEM((ROWS, 512), BF16),
-            pltpu.VMEM((4, 4, ROWS, 256), BF16),
-            pltpu.VMEM((4, 4, ROWS, 256), BF16),
-            pltpu.VMEM((4, 4, ROWS, 128), BF16),
-            pltpu.VMEM((4, 4, ROWS, 128), BF16),
-            pltpu.VMEM((4, 4, ROWS, 128), BF16),
-            pltpu.VMEM((4, 4, ROWS, 128), BF16),
+            pltpu.VMEM((2, 4, 4, ROWS, 256), BF16),
+            pltpu.VMEM((2, 4, 4, ROWS, 128), BF16),
+            pltpu.VMEM((2, 4, 4, ROWS, 128), BF16),
             pltpu.VMEM((4, ROWS, 128), F32),
             pltpu.VMEM((4, ROWS, 128), F32),
             pltpu.VMEM((4, ROWS, 128), F32),
@@ -527,7 +740,8 @@
         compiler_params=pltpu.CompilerParams(
             collective_id=0, has_side_effects=True, vmem_limit_bytes=67043328),
     )(tokens_in[0], user_ids, w_in, w_out, cotangent[0])
-    return output[None], grad_tokens[None], total_in, total_out.T
+    output, grad_tokens, total_in, total_out = finish(output, grad_tokens, total_in, total_out)
+    return output, grad_tokens, total_in, total_out.T
 
 
 def solution(mesh):

time: 135 us -> 102 us (0.76)
  Pallas kernels: 128 us -> 100 us
  local copies, waits for them, and re-layouts: 5.8 us -> 0 us
    pallas_call x1, Pallas kernels: 128 us -> 98 us  [local(): pl.pallas_call(layer_kernel, name='layer', out_shape=(jax.ShapeDtypeStruc...]
    unnamed x8 -> x0, local copies, waits for them, and re-layouts: 5.8 us -> none
    pallas_call x0 -> x1, Pallas kernels: none -> 2.46 us  [finish(): pl.pallas_call(finish_kernel, name='finish', out_shape=(jax.ShapeDtypeStr...]
where the time goes in v2:
time: 102 us; the launch traced here: 101 us
  Pallas kernels  100 us (98%)
    pallas_call x1, Pallas kernels, local(): pl.pallas_call(layer_kernel, name='layer', out_shape=(jax.ShapeDtypeStruc...  98 us
    pallas_call x1, Pallas kernels, finish(): pl.pallas_call(finish_kernel, name='finish', out_shape=(jax.ShapeDtypeStr...  2.46 us

profile of v2, /device:TPU:0, one launch (start us, length us, event | category | flops | bytes accessed | tf_op | source)
XLA Modules:
  0.0 101.3 jit_solution(1768797400051393012)
XLA Ops:
  0.6 98.0 %layer.1 = (bf16[512,1024]{1,0:T(8,128)(2,1)}, bf16[512,1024]{1,0:T(8,128)(2,1)}, f32[8,2048]{1,0:T(8,128)}, f32[8,512]{1,0:T(8,128)}) custom-call(bf16[512,1024]{1,0:T(8,128)(2,1)} %bitcast.3, s32[1,4096]{1,0:T(1,128)} %ids.1, bf16[1024,2048]{1,0:T(8,128)(2,1)} %w_in_hbm.1, bf16[512,1024]{1,0:T(8,128)(2,1)} %w_out_hbm.1, bf16[512,1024]{1,0:T(8,128)(2,1)} %bitcast.4), custom_call_target="tpu_custom_call" | custom-call | tf_op jit(solution)/shard_map/layer/pallas_call | solution.py:688
  98.7 2.5 %finish.1 = (bf16[1,512,1024]{2,1,0:T(8,128)(2,1)}, bf16[1,512,1024]{2,1,0:T(8,128)(2,1)}, f32[8,2048]{1,0:T(8,128)}, f32[8,512]{1,0:T(8,128)}) custom-call(bf16[512,1024]{1,0:T(8,128)(2,1)} %get-tuple-element.12.a, bf16[512,1024]{1,0:T(8,128)(2,1)} %get-tuple-element.13.b, f32[8,2048]{1,0:T(8,128)} %get-tuple-element.14.p, f32[8,512]{1,0:T(8,128)} %get-tuple-element.15.q), custom_call_target="tpu_custom_call" | custom-call | tf_op jit(solution)/shard_map/finish/pallas_call | solution.py:659

commit v3 on v2

--- a/solution.py
+++ b/solution.py
@@ -16,25 +16,26 @@
 HALF_SCALE = 0.5 / math.sqrt(HD)
 MESH = pl.DeviceIdType.MESH
 NB = 5
+GROUPS = ((0, 2), (2, 1), (3, 2))
 
 OWN_MOVES = (
     (0, 1, 0, (0, 1, 2, 3)),
-    (0, 3, 0, (2, 3)),
-    (1, 2, 1, (0, 1, 2)),
-    (1, 0, 1, (3, 1, 2)),
+    (0, 3, 0, (0, 1)),
+    (1, 2, 1, (1, 2, 3)),
+    (1, 0, 1, (0, 1, 2)),
     (2, 3, 2, (0, 1, 2, 3)),
 )
 RELAYS = {
-    (1, 0, 0): 2, (1, 0, 1): 2,
-    (0, 1, 3): 3, (0, 1, 1): 3, (0, 1, 2): 3,
-    (3, 0, 2): 2, (3, 0, 3): 2, (3, 1, 3): 2,
-    (2, 1, 0): 3,
+    (1, 0, 2): 2, (1, 0, 3): 2,
+    (0, 1, 0): 3, (0, 1, 1): 3, (0, 1, 2): 3,
+    (3, 0, 0): 2, (3, 0, 1): 2, (3, 1, 0): 2,
+    (2, 1, 3): 3,
 }
 ARRIVALS = {
-    0: ((1, 3), (1, 1), (1, 2)),
+    0: ((1, 0), (1, 1), (1, 2)),
     1: ((0, 0), (0, 1), (0, 2), (0, 3)),
-    2: ((1, 0), (1, 1), (0, 2), (1, 2), (0, 3), (0, 0), (1, 3), (0, 1)),
-    3: ((2, 0), (0, 2), (2, 1), (0, 3), (2, 2), (1, 3), (2, 3), (1, 1), (1, 2), (1, 0)),
+    2: ((1, 1), (0, 0), (1, 2), (0, 1), (1, 3), (1, 0), (0, 2), (0, 3)),
+    3: ((2, 0), (0, 0), (2, 1), (0, 1), (2, 2), (1, 0), (2, 3), (1, 1), (1, 2), (1, 3)),
 }
 STEPS = 10
 QUERY_MOVES = (
@@ -58,10 +59,10 @@
     3: ((0, 2), (0, 3), (2, 0), (2, 1), (2, 2), (2, 3), (1, 0), (1, 1), (1, 3), (1, 2)),
 }
 GRAD_ARRIVALS = {
-    0: ((1, 3), (1, 1), (1, 2)),
+    0: ((1, 0), (1, 1), (1, 2)),
     1: ((0, 0), (0, 1), (0, 2), (0, 3)),
-    2: ((1, 0), (1, 1), (0, 2), (1, 2), (0, 0), (0, 3), (0, 1), (1, 3)),
-    3: ((2, 0), (2, 1), (0, 2), (2, 2), (0, 3), (2, 3), (1, 3), (1, 1), (1, 0), (1, 2)),
+    2: ((1, 1), (1, 2), (0, 0), (1, 3), (0, 2), (0, 1), (0, 3), (1, 0)),
+    3: ((2, 0), (2, 1), (0, 0), (2, 2), (0, 1), (2, 3), (1, 0), (1, 1), (1, 3), (1, 2)),
 }
 
 
@@ -102,27 +103,38 @@
         self.ss, self.rs, self.sp, self.rp = sems
         self.chip, self.core, self.target = chip, core, target
         self.moves, self.relays, self.arrivals = moves, relays, arrivals
+        self.sent = {}
+        for role in range(4):
+            mine = [(receiver, owner, h) for sender, receiver, owner, heads in moves if sender == role for h in heads]
+            mine += [(receiver, owner, h) for (sender, owner, h), receiver in relays.items() if sender == role]
+            for k, (receiver, owner, h) in enumerate(mine):
+                self.sent[role, receiver, owner, h] = k
 
     def move(self, sender, receiver, owner, h):
-        k = 0 if receiver == sender + 1 else 1
-        return remote(self.near.at[owner, h], self.near.at[owner, h], self.ss.at[owner, h, k],
-                      self.rs.at[owner, h], self.target(receiver, self.core))
+        return remote(self.near.at[owner, h], self.near.at[owner, h], self.ss.at[self.sent[sender, receiver, owner, h]],
+                      self.rs.at[self.arrivals[receiver].index((owner, h))], self.target(receiver, self.core))
+
+    def landed(self, step, owner, h):
+        here = self.near.at[owner, h]
+        return remote(here, here, self.ss.at[0], self.rs.at[step], self.target(turn(self.chip, 1), self.core))
 
     def share(self, owner, h):
-        return remote(self.near.at[owner, h], self.far.at[owner, h], self.sp.at[owner, h],
-                      self.rp.at[owner, h], self.target(self.chip, 1 - self.core))
-
-    def start(self, moves=None, share=True):
+        k = jnp.where(self.chip - owner == 1, 4, 0) + h
+        return remote(self.near.at[owner, h], self.far.at[owner, h], self.sp.at[k],
+                      self.rp.at[k], self.target(self.chip, 1 - self.core))
+
+    def start(self, moves=None, share=True, only=(0, 1, 2, 3)):
         if share:
             @pl.when(self.core == 0)
             def _():
-                for h in range(HEADS):
+                for h in only:
                     self.share(self.chip, h).start()
         for sender, receiver, owner, heads in (self.moves if moves is None else moves):
             @pl.when(self.chip == sender)
             def _():
                 for h in heads:
-                    self.move(sender, receiver, owner, h).start()
+                    if h in only:
+                        self.move(sender, receiver, owner, h).start()
 
     def arrive(self, step, roles=(0, 1, 2, 3)):
         for role in roles:
@@ -133,7 +145,7 @@
 
             @pl.when(self.chip == role)
             def _():
-                self.move(role, (role + 1) % 4, owner, h).wait_recv()
+                self.landed(step, owner, h).wait_recv()
                 if (role, owner, h) in self.relays:
                     self.move(role, self.relays[role, owner, h], owner, h).start()
                 if owner == role - 1:
@@ -147,12 +159,16 @@
         code = jnp.int32(-1)
         for role, order in self.arrivals.items():
             for k, (owner, h) in enumerate(order):
-                value = (self.relays.get((role, owner, h), -1) + 1) * 16 + owner * 4 + h
+                dest = self.relays.get((role, owner, h), -1)
+                value = owner * 4 + h
+                if dest >= 0:
+                    there = self.arrivals[dest].index((owner, h))
+                    value += 16 * (dest + 1) + 128 * there + 2048 * self.sent[role, dest, owner, h]
                 code = jnp.where((self.chip == role) & (step == k), value, code)
-        return code >= 0, (code // 4) % 4, code % 4, code // 16 - 1
+        return (code >= 0, (code // 4) % 4, code % 4, (code // 16) % 8 - 1, (code // 128) % 16, code // 2048)
 
     def service(self, step, serve=None):
-        wanted, owner, h, dest = self.look(step)
+        wanted, owner, h, dest, there, k = self.look(step)
         if serve is not None:
             wanted = wanted & serve
 
@@ -160,14 +176,11 @@
         def _():
             here = self.near.at[owner, h]
             gap = self.chip - owner
-            remote(here, here, self.ss.at[owner, h, 0], self.rs.at[owner, h],
-                   self.target(turn(self.chip, 1), self.core)).wait_recv()
+            self.landed(step, owner, h).wait_recv()
 
             @pl.when(dest >= 0)
             def _():
-                k = jnp.where(dest == self.chip + 1, 0, 1)
-                remote(here, here, self.ss.at[owner, h, k], self.rs.at[owner, h],
-                       self.target(dest, self.core)).start()
+                remote(here, here, self.ss.at[k], self.rs.at[there], self.target(dest, self.core)).start()
 
             @pl.when((gap == 1) | ((gap == 2) & (self.core == 1)))
             def _():
@@ -199,11 +212,11 @@
                         self.share(owner, h).wait_send()
 
 
-def layer_kernel(tokens_hbm, ids, w_in_hbm, w_out_hbm, cot_hbm, output_hbm, grad_tokens_hbm, out_in, out_out,
-                 output, grad_tokens, out_sems, tokens, w_in, w_out, cot, in_sems, normed_t, cot_t, normed, slope, u, kv, qs, gs, att, dq, dk, dv, gated, gh, masks, masks_t,
-                 tmp, part, s2, recv1, r2a, r2b, s3a, s3b, r3a, r3b, t4, r4,
-                 kss, krs, ksp, krp, qss, qrs, qsp, qrp, gss, grs, gsp, grp,
-                 ss1, rs1, ss2, rs2, ss3, rs3, ss4, rs4):
+def layer_kernel(tokens_hbm, ids, w_in_hbm, w_out_hbm, cot_hbm, output_hbm, grad_tokens_hbm, out_in_hbm, out_out_hbm,
+                 out_in, out_out, output, grad_tokens, out_sems, tokens, w_in, w_out, cot, in_sems, normed_t, cot_t, normed, slope, u, kv, qs, gs, att, dq, dk, dv, gated, gh, masks, masks_t,
+                 tmp, part, s2, recv1, r2, s3a, s3b, r3a, r3b, t4, r4,
+                 kss, krs, ksp, krp, qss, qrs, qsp, qrp, grs, grp,
+                 ss1, rs1, sss, rs2, rs3, rs4):
     y, x, z, c = place()
     other = 1 - c
     block = z * 2 + c
@@ -235,7 +248,7 @@
                     OWN_MOVES, RELAYS, ARRIVALS)
     queries = Gather(qs, (qss, qrs, qsp, qrp), mz, mc, mirrored,
                      QUERY_MOVES, QUERY_RELAYS, QUERY_ARRIVALS)
-    grads = Gather(gs, (gss, grs, gsp, grp), mz, mc, mirrored,
+    grads = Gather(gs, (kss, grs, ksp, grp), mz, mc, mirrored,
                    OWN_MOVES, RELAYS, GRAD_ARRIVALS)
 
     def stats(v):
@@ -256,23 +269,19 @@
     def _(rows):
         normed[rows, :] = stats(tokens[rows, :].astype(F32))[0].astype(BF16)
 
-    def features(col, put):
-        w_ins[col].wait()
-
+    def features(col, width, put):
         @row_loop(256)
         def _(rows):
-            half = 0.5 * dot_nn(normed[rows, :], w_in[:, col:col + 512])
+            half = 0.5 * dot_nn(normed[rows, :], w_in[:, col:col + width])
             t = jnp.tanh(half)
-            slope[rows, col:col + 512] = 0.5 * (1.0 + t) * (1.0 + half * (1.0 - t))
+            slope[rows, col:col + width] = 0.5 * (1.0 + t) * (1.0 + half * (1.0 - t))
             put(rows, (half * (1.0 + t)).astype(BF16))
 
-    def put_k(rows, a):
-        for h in range(HEADS):
-            kv[0, z, h, rows, 0:128] = a[:, h * 128:(h + 1) * 128]
-
-    def put_v(rows, a):
-        for h in range(HEADS):
-            kv[0, z, h, rows, 128:256] = a[:, h * 128:(h + 1) * 128]
+    def put_kv(first, at):
+        def put(rows, a):
+            for h in range(2):
+                kv[0, z, first + h, rows, at:at + 128] = a[:, h * 128:(h + 1) * 128]
+        return put
 
     def put_q(rows, a):
         for h in range(HEADS):
@@ -281,13 +290,20 @@
     def put_u(rows, a):
         u[rows, :] = a
 
-    features(1536, put_k)
-    features(512, put_v)
+    w_ins[1536].wait()
+    features(1536, 256, put_kv(0, 0))
+    w_ins[512].wait()
+    features(512, 256, put_kv(0, 128))
     pl.semaphore_wait(barrier, len(peers))
-    before.start()
-    features(1024, put_q)
+    before.start(only=(0, 1))
+    features(1792, 256, put_kv(2, 0))
+    features(768, 256, put_kv(2, 128))
+    before.start(only=(2, 3))
+    w_ins[1024].wait()
+    features(1024, 512, put_q)
     queries.start(QUERY_MOVES[:4])
-    features(0, put_u)
+    w_ins[0].wait()
+    features(0, 512, put_u)
 
     def ids_of(b):
         b = jnp.clip(b, 0, 7)
@@ -397,7 +413,7 @@
         pipeline(items, scores, weigh, add)
 
     def meet(gather, step, compute, flip, also=None):
-        there, o, h, _ = gather.look(step)
+        there, o, h, _, _, _ = gather.look(step)
         gap = gather.chip - o
         even = 2 * gap
         odd = even + 2 * gather.core - 1
@@ -438,57 +454,91 @@
             s2[b, r] = tmp[:, other].reshape(4, 32, 512).astype(BF16)
         pair_copy(b).start()
 
-    def plane_copies(b):
+    def plane_copies(g):
+        b = pl.ds(*GROUPS[g])
         out = []
         for d in (1, 2, 3):
             xx, yy = turn(x, d), turn(y, d)
-            out.append(remote(s2.at[b, :, xx, :, pl.ds(0, 256)], r2a.at[b, d - 1], ss2.at[b, d - 1],
-                              rs2.at[b, d - 1], device(y, xx, z, c)))
-            out.append(remote(s2.at[b, yy, :, :, pl.ds(256, 256)], r2b.at[b, d - 1], ss2.at[b, d + 2],
-                              rs2.at[b, d + 2], device(yy, x, z, c)))
+            out.append(remote(s2.at[b, :, xx, :, pl.ds(0, 256)], r2.at[0, d - 1, b], sss.at[g, d - 1],
+                              rs2.at[g, d - 1], device(y, xx, z, c)))
+            out.append(remote(s2.at[b, yy, :, :, pl.ds(256, 256)], r2.at[1, d - 1, b], sss.at[g, d + 2],
+                              rs2.at[g, d + 2], device(yy, x, z, c)))
         return out
 
-    def line_copies(b):
+    def line_copies(g):
+        b = pl.ds(*GROUPS[g])
         out = []
         for d in (1, 2, 3):
             xx, yy = turn(x, d), turn(y, d)
-            out.append(remote(s3a.at[b, yy], r3a.at[b, d - 1], ss3.at[b, d - 1], rs3.at[b, d - 1],
+            out.append(remote(s3a.at[b, yy], r3a.at[d - 1, b], sss.at[g, d - 1], rs3.at[g, d - 1],
                               device(yy, x, z, c)))
-            out.append(remote(s3b.at[b, xx], r3b.at[b, d - 1], ss3.at[b, d + 2], rs3.at[b, d + 2],
+            out.append(remote(s3b.at[b, xx], r3b.at[d - 1, b], sss.at[g, d + 2], rs3.at[g, d + 2],
                               device(y, xx, z, c)))
         return out
 
-    def second(b):
-        pair_copy(b).wait()
-        for i in range(4):
-            mine = part[b, i * 128:(i + 1) * 128, :].reshape(4, 32, 512)
-            s2[b, i] = (mine + recv1[b, i].astype(F32)).astype(BF16)
-        for cp in plane_copies(b):
+    def chip_copies(g):
+        b = pl.ds(*GROUPS[g])
+        return [remote(t4.at[turn(z, d), b], r4.at[d - 1, b], sss.at[g, d - 1], rs4.at[g, d - 1],
+                       device(y, x, turn(z, d), c)) for d in (1, 2, 3)]
+
+    def blocks_of(g):
+        return range(GROUPS[g][0], GROUPS[g][0] + GROUPS[g][1])
+
+    def second(g):
+        for b in blocks_of(g):
+            pair_copy(b).wait()
+            for i in range(4):
+                mine = part[b, i * 128:(i + 1) * 128, :].reshape(4, 32, 512)
+                s2[b, i] = (mine + recv1[b, i].astype(F32)).astype(BF16)
+        for cp in plane_copies(g):
             cp.start()
 
-    def third(b):
-        for cp in plane_copies(b):
+    def third(g):
+        for cp in plane_copies(g):
             cp.wait()
-        a = s2[b, :, x, :, 0:256].astype(F32)
-        e = s2[b, y, :, :, 256:512].astype(F32)
-        for d in range(3):
-            a = a + r2a[b, d].astype(F32)
-            e = e + r2b[b, d].astype(F32)
-        s3a[b] = a.astype(BF16)
-        s3b[b] = e.astype(BF16)
-        for cp in line_copies(b):
+        for b in blocks_of(g):
+            a = s2[b, :, x, :, 0:256].astype(F32)
+            e = s2[b, y, :, :, 256:512].astype(F32)
+            for d in range(3):
+                a = a + r2[0, d, b].astype(F32)
+                e = e + r2[1, d, b].astype(F32)
+            s3a[b] = a.astype(BF16)
+            s3b[b] = e.astype(BF16)
+        for cp in line_copies(g):
             cp.start()
 
-    def fourth(b):
-        for cp in line_copies(b):
+    def fourth(g):
+        for cp in line_copies(g):
             cp.wait()
-        a = s3a[b, y].astype(F32)
-        e = s3b[b, x].astype(F32)
-        for d in range(3):
-            a = a + r3a[b, d].astype(F32)
-            e = e + r3b[b, d].astype(F32)
-        t4[:, :, b * 512:b * 512 + 256] = a.reshape(4, 8, 256)
-        t4[:, :, b * 512 + 256:b * 512 + 512] = e.reshape(4, 8, 256)
+        for b in blocks_of(g):
+            a = s3a[b, y].astype(F32)
+            e = s3b[b, x].astype(F32)
+            for d in range(3):
+                a = a + r3a[d, b].astype(F32)
+                e = e + r3b[d, b].astype(F32)
+            t4[:, b, :, 0:256] = a.reshape(4, 8, 256)
+            t4[:, b, :, 256:512] = e.reshape(4, 8, 256)
+        for cp in chip_copies(g):
+            cp.start()
+
+    RESULT = {1: 0, 2: 1024, 3: 512, 4: 1536}
+
+    def result_copy(b):
+        if b == 0:
+            return pltpu.make_async_copy(out_out, out_out_hbm, out_sems.at[2])
+        cols = pl.ds(RESULT[b], 512)
+        return pltpu.make_async_copy(out_in.at[:, cols], out_in_hbm.at[:, cols], out_sems.at[2 + b])
+
+    def fifth(g):
+        for cp in chip_copies(g):
+            cp.wait()
+        for b in blocks_of(g):
+            total = t4[z, b] + r4[0, b] + r4[1, b] + r4[2, b]
+            if b == 0:
+                out_out[...] = total
+            else:
+                out_in[:, RESULT[b]:RESULT[b] + 512] = total
+            result_copy(b).start()
 
     forward_tiles(tiles((0, z), False, range(HEADS), 0), first=True)
     cot_in.wait()
@@ -502,7 +552,6 @@
     beside(before, forward_tiles, False)
     before.service(0)
     before.service(1)
-    queries.start(QUERY_MOVES[4:5], share=False)
     for step in range(2):
         queries.arrive(step, roles=(1, 2, 3))
 
@@ -513,7 +562,7 @@
 
         @pl.when(step == 3)
         def _():
-            queries.start(QUERY_MOVES[5:], share=False)
+            queries.start(QUERY_MOVES[4:], share=False)
 
 
     @row_loop(256)
@@ -533,28 +582,31 @@
         for h in range(HEADS):
             gs[0, mz, h, rows, :] = back[:, h * 128:(h + 1) * 128]
 
+    before.drain()
     grads.start()
     output_out = pltpu.make_async_copy(output, output_hbm, out_sems.at[0])
     output_out.start()
+    queries.arrive(0, roles=(0,))
+    queries.arrive(1, roles=(0,))
     query_tiles(tiles((0, z), False, range(HEADS), 0), first=True)
     weight(0, cot_t, gated[...])
     weight(1, normed_t, gh[:, 0:512])
-    queries.arrive(0, roles=(0,))
-    queries.arrive(1, roles=(0,))
     queries.arrive(2, roles=(1,))
     early = mz < 2
 
     @pl.loop(1, 5)
     def _(d):
-        grads.service(d - 1, serve=early)
-
         @pl.when(block >= d)
         def _():
             owner = jnp.where(d % 2 == 0, z - d // 2, z - (d + 1) // 2 + c)
             query_tiles(tiles((d % 2, owner), False, range(HEADS), d))
 
-    second(0)
-    second(1)
+        grads.service(d - 1, serve=early)
+
+        @pl.when(d == 2)
+        def _():
+            second(0)
+
     queries.arrive(3, roles=(1,))
 
     @row_loop(256)
@@ -563,22 +615,27 @@
             at = 1024 + h * 128
             gh[rows, at:at + 128] = (dq[h, rows, :] * HALF_SCALE * slope[rows, at:at + 128]).astype(BF16)
 
-    weight(3, normed_t, gh[:, 1024:1536])
+    weight(2, normed_t, gh[:, 1024:1536])
     key_tiles(tiles((0, mz), True, range(HEADS), 0), first=True)
     beside(grads, key_tiles, True, also=queries)
-    second(3)
+    second(1)
     third(0)
-    third(1)
     late = mz >= 2
     grads.service(0, serve=late)
     for step in range(2, 8):
         queries.arrive(step, roles=(2,))
-    for step in range(2, STEPS):
+    for step in range(2, 8):
         queries.arrive(step, roles=(3,))
 
     @pl.loop(0, STEPS)
     def _(step):
         grads.service(step + 1, serve=late)
+
+        @pl.when(step == 4)
+        def _():
+            queries.arrive(8, roles=(3,))
+            queries.arrive(9, roles=(3,))
+
         meet(grads, step, key_tiles, True, also=queries)
 
     @row_loop(256)
@@ -589,11 +646,10 @@
             at = 1536 + h * 128
             gh[rows, at:at + 128] = (dk[h, rows, :] * HALF_SCALE * slope[rows, at:at + 128]).astype(BF16)
 
-    weight(2, normed_t, gh[:, 512:1024])
+    weight(3, normed_t, gh[:, 512:1024])
     weight(4, normed_t, gh[:, 1536:2048])
-    third(3)
+    third(1)
     second(2)
-    second(4)
 
     @row_loop(256)
     def _(rows):
@@ -607,27 +663,17 @@
     tokens_out.start()
     fourth(0)
     fourth(1)
-    fourth(3)
     third(2)
-    third(4)
+    fifth(0)
+    fifth(1)
     fourth(2)
-    fourth(4)
-    last = []
-    for d in (1, 2, 3):
-        zz = turn(z, d)
-        cp = remote(t4.at[zz], r4.at[d - 1], ss4.at[d - 1], rs4.at[d - 1], device(y, x, zz, c))
-        cp.start()
-        last.append(cp)
-    before.drain()
     queries.drain()
     grads.drain()
     output_out.wait()
     tokens_out.wait()
-    for cp in last:
-        cp.wait()
-    total = t4[z] + r4[0] + r4[1] + r4[2]
-    out_out[...] = total[:, 0:512]
-    out_in[...] = total[:, 512:2560]
+    fifth(2)
+    for b in range(NB):
+        result_copy(b).wait()
 
 
 def finish_kernel(a, b, p, q, out_a, out_b, out_p, out_q, va, vb, vp, vq, ins, outs):
@@ -682,9 +728,6 @@
     hbm = pl.BlockSpec(memory_space=pl.ANY)
     dma = pltpu.SemaphoreType.DMA
 
-    def gather_sems():
-        return [dma((4, 4, 2)), dma((4, 4)), dma((4, 4)), dma((4, 4))]
-
     output, grad_tokens, total_in, total_out = pl.pallas_call(
         layer_kernel,
         name="layer",
@@ -695,11 +738,13 @@
             jax.ShapeDtypeStruct((8, 512), F32),
         ),
         in_specs=[hbm, vmem, hbm, hbm, hbm],
-        out_specs=(hbm, hbm, vmem, vmem),
+        out_specs=(hbm,) * 4,
         scratch_shapes=[
+            pltpu.VMEM((8, 2048), F32),
+            pltpu.VMEM((8, 512), F32),
             pltpu.VMEM((ROWS, 1024), BF16),
             pltpu.VMEM((ROWS, 1024), BF16),
-            dma((2,)),
+            dma((7,)),
             pltpu.VMEM((ROWS, 1024), BF16),
             pltpu.VMEM((1024, 2048), BF16),
             pltpu.VMEM((512, 1024), BF16),
@@ -725,17 +770,17 @@
             pltpu.VMEM((NB, 512, 512), F32),
             pltpu.VMEM((NB, 4, 4, 32, 512), BF16),
             pltpu.VMEM((NB, 4, 4, 32, 512), BF16),
-            pltpu.VMEM((NB, 3, 4, 32, 256), BF16),
-            pltpu.VMEM((NB, 3, 4, 32, 256), BF16),
+            pltpu.VMEM((2, 3, NB, 4, 32, 256), BF16),
             pltpu.VMEM((NB, 4, 32, 256), BF16),
             pltpu.VMEM((NB, 4, 32, 256), BF16),
-            pltpu.VMEM((NB, 3, 32, 256), BF16),
-            pltpu.VMEM((NB, 3, 32, 256), BF16),
-            pltpu.VMEM((4, 8, NB * 512), F32),
-            pltpu.VMEM((3, 8, NB * 512), F32),
-            *gather_sems(), *gather_sems(), *gather_sems(),
-            dma((NB,)), dma((NB,)), dma((NB, 6)), dma((NB, 6)), dma((NB, 6)), dma((NB, 6)),
-            dma((3,)), dma((3,)),
+            pltpu.VMEM((3, NB, 32, 256), BF16),
+            pltpu.VMEM((3, NB, 32, 256), BF16),
+            pltpu.VMEM((4, NB, 8, 512), F32),
+            pltpu.VMEM((3, NB, 8, 512), F32),
+            dma((9,)), dma((10,)), dma((8,)), dma((8,)),
+            dma((8,)), dma((10,)), dma((8,)), dma((8,)),
+            dma((10,)), dma((8,)),
+            dma((NB,)), dma((NB,)), dma((3, 6)), dma((3, 6)), dma((3, 6)), dma((3, 3)),
         ],
         compiler_params=pltpu.CompilerParams(
             collective_id=0, has_side_effects=True, vmem_limit_bytes=67043328),

time: 102 us -> 97 us (0.951)
  Pallas kernels: 100 us -> 95.9 us
    pallas_call x1, Pallas kernels: 98 us -> 93.5 us  [local(): pl.pallas_call(layer_kernel, name='layer', out_shape=(jax.ShapeDtypeStruc...]
where the time goes in v3:
time: 97 us; the launch traced here: 96.8 us
  Pallas kernels  95.9 us (99%)
    pallas_call x1, Pallas kernels, local(): pl.pallas_call(layer_kernel, name='layer', out_shape=(jax.ShapeDtypeStruc...  93.5 us
    pallas_call x1, Pallas kernels, finish(): pl.pallas_call(finish_kernel, name='finish', out_shape=(jax.ShapeDtypeStr...  2.46 us

profile of v3, /device:TPU:0, one launch (start us, length us, event | category | flops | bytes accessed | tf_op | source)
XLA Modules:
  0.0 96.8 jit_solution(7518707307149947972)
XLA Ops:
  0.6 93.5 %layer.1 = (bf16[512,1024]{1,0:T(8,128)(2,1)}, bf16[512,1024]{1,0:T(8,128)(2,1)}, f32[8,2048]{1,0:T(8,128)}, f32[8,512]{1,0:T(8,128)}) custom-call(bf16[512,1024]{1,0:T(8,128)(2,1)} %bitcast.3, s32[1,4096]{1,0:T(1,128)} %ids.1, bf16[1024,2048]{1,0:T(8,128)(2,1)} %w_in_hbm.1, bf16[512,1024]{1,0:T(8,128)(2,1)} %w_out_hbm.1, bf16[512,1024]{1,0:T(8,128)(2,1)} %bitcast.4), custom_call_target="tpu_custom_call" | custom-call | tf_op jit(solution)/shard_map/layer/pallas_call | solution.py:731
  94.1 2.5 %finish.1 = (bf16[1,512,1024]{2,1,0:T(8,128)(2,1)}, bf16[1,512,1024]{2,1,0:T(8,128)(2,1)}, f32[8,2048]{1,0:T(8,128)}, f32[8,512]{1,0:T(8,128)}) custom-call(bf16[512,1024]{1,0:T(8,128)(2,1)} %get-tuple-element.12.a, bf16[512,1024]{1,0:T(8,128)(2,1)} %get-tuple-element.13.b, f32[8,2048]{1,0:T(8,128)} %get-tuple-element.14.p, f32[8,512]{1,0:T(8,128)} %get-tuple-element.15.q), custom_call_target="tpu_custom_call" | custom-call | tf_op jit(solution)/shard_map/finish/pallas_call | solution.py:705

commit v4 on v3

--- a/solution.py
+++ b/solution.py
@@ -214,7 +214,7 @@
 
 def layer_kernel(tokens_hbm, ids, w_in_hbm, w_out_hbm, cot_hbm, output_hbm, grad_tokens_hbm, out_in_hbm, out_out_hbm,
                  out_in, out_out, output, grad_tokens, out_sems, tokens, w_in, w_out, cot, in_sems, normed_t, cot_t, normed, slope, u, kv, qs, gs, att, dq, dk, dv, gated, gh, masks, masks_t,
-                 tmp, part, s2, recv1, r2, s3a, s3b, r3a, r3b, t4, r4,
+                 part, s2, recv1, r2, s3a, s3b, r3a, r3b, t4, r4,
                  kss, krs, ksp, krp, qss, qrs, qsp, qrp, grs, grp,
                  ss1, rs1, sss, rs2, rs3, rs4):
     y, x, z, c = place()
@@ -445,13 +445,14 @@
         return remote(s2.at[b], recv1.at[b], ss1.at[b], rs1.at[b], device(y, x, z, other))
 
     def weight(b, left, cols):
-        @pl.loop(0, 4)
-        def _(r):
-            rows = pl.ds(pl.multiple_of(r * 256, 256), 256)
-            tmp[...] = dot_nn(left[rows, :], cols).reshape(16, 2, 8, 512)
-            half = pl.ds(pl.multiple_of(r * 128, 128), 128)
-            part[b, half, :] = tmp[:, c].reshape(128, 512)
-            s2[b, r] = tmp[:, other].reshape(4, 32, 512).astype(BF16)
+        ahead = dot_nn(left[0:256, :], cols)
+        for r in range(4):
+            now = ahead.reshape(16, 2, 8, 512)
+            if r < 3:
+                ahead = dot_nn(left[(r + 1) * 256:(r + 2) * 256, :], cols)
+            even, odd = now[:, 0].reshape(128, 512), now[:, 1].reshape(128, 512)
+            part[b, r * 128:(r + 1) * 128, :] = jnp.where(c == 0, even, odd)
+            s2[b, r] = jnp.where(c == 0, odd, even).reshape(4, 32, 512).astype(BF16)
         pair_copy(b).start()
 
     def plane_copies(g):
@@ -572,7 +573,6 @@
         uu = u[rows, :].astype(F32)
         g = (no * uu).astype(BF16)
         gated[rows, :] = g
-        output[rows, :] = (dot_nn(g, w_out[...]) + tokens[rows, :].astype(F32)).astype(BF16)
         gg = dot_nt(cot[rows, :], w_out[...])
         gh[rows, 0:512] = (gg * no * slope[rows, 0:512]).astype(BF16)
         gn = gg * uu
@@ -582,10 +582,8 @@
         for h in range(HEADS):
             gs[0, mz, h, rows, :] = back[:, h * 128:(h + 1) * 128]
 
-    before.drain()
+    pl.when(mz < 3)(before.drain)
     grads.start()
-    output_out = pltpu.make_async_copy(output, output_hbm, out_sems.at[0])
-    output_out.start()
     queries.arrive(0, roles=(0,))
     queries.arrive(1, roles=(0,))
     query_tiles(tiles((0, z), False, range(HEADS), 0), first=True)
@@ -619,8 +617,8 @@
     key_tiles(tiles((0, mz), True, range(HEADS), 0), first=True)
     beside(grads, key_tiles, True, also=queries)
     second(1)
-    third(0)
     late = mz >= 2
+    pl.when(mz == 3)(before.drain)
     grads.service(0, serve=late)
     for step in range(2, 8):
         queries.arrive(step, roles=(2,))
@@ -630,6 +628,10 @@
     @pl.loop(0, STEPS)
     def _(step):
         grads.service(step + 1, serve=late)
+
+        @pl.when(step == 3)
+        def _():
+            third(0)
 
         @pl.when(step == 4)
         def _():
@@ -663,6 +665,13 @@
     tokens_out.start()
     fourth(0)
     fourth(1)
+
+    @row_loop(256)
+    def _(rows):
+        output[rows, :] = (dot_nn(gated[rows, :], w_out[...]) + tokens[rows, :].astype(F32)).astype(BF16)
+
+    output_out = pltpu.make_async_copy(output, output_hbm, out_sems.at[0])
+    output_out.start()
     third(2)
     fifth(0)
     fifth(1)
@@ -766,7 +775,6 @@
             pltpu.VMEM((ROWS, 2048), BF16),
             pltpu.VMEM((5, ROWS, ROWS), BF16),
             pltpu.VMEM((5, ROWS, ROWS), BF16),
-            pltpu.VMEM((16, 2, 8, 512), F32),
             pltpu.VMEM((NB, 512, 512), F32),
             pltpu.VMEM((NB, 4, 4, 32, 512), BF16),
             pltpu.VMEM((NB, 4, 4, 32, 512), BF16),

time: 97 us -> 94.3 us (0.972)
  Pallas kernels: 95.9 us -> 93.2 us
    pallas_call x1, Pallas kernels: 93.5 us -> 90.8 us  [local(): pl.pallas_call(layer_kernel, name='layer', out_shape=(jax.ShapeDtypeStruc...]
where the time goes in v4:
time: 94.3 us; the launch traced here: 94 us
  Pallas kernels  93.2 us (99%)
    pallas_call x1, Pallas kernels, local(): pl.pallas_call(layer_kernel, name='layer', out_shape=(jax.ShapeDtypeStruc...  90.8 us
    pallas_call x1, Pallas kernels, finish(): pl.pallas_call(finish_kernel, name='finish', out_shape=(jax.ShapeDtypeStr...  2.46 us

profile of v4, /device:TPU:0, one launch (start us, length us, event | category | flops | bytes accessed | tf_op | source)
XLA Modules:
  0.0 94.0 jit_solution(13286341990764756728)
XLA Ops:
  0.6 90.8 %layer.1 = (bf16[512,1024]{1,0:T(8,128)(2,1)}, bf16[512,1024]{1,0:T(8,128)(2,1)}, f32[8,2048]{1,0:T(8,128)}, f32[8,512]{1,0:T(8,128)}) custom-call(bf16[512,1024]{1,0:T(8,128)(2,1)} %bitcast.3, s32[1,4096]{1,0:T(1,128)} %ids.1, bf16[1024,2048]{1,0:T(8,128)(2,1)} %w_in_hbm.1, bf16[512,1024]{1,0:T(8,128)(2,1)} %w_out_hbm.1, bf16[512,1024]{1,0:T(8,128)(2,1)} %bitcast.4), custom_call_target="tpu_custom_call" | custom-call | tf_op jit(solution)/shard_map/layer/pallas_call | solution.py:740
  91.4 2.5 %finish.1 = (bf16[1,512,1024]{2,1,0:T(8,128)(2,1)}, bf16[1,512,1024]{2,1,0:T(8,128)(2,1)}, f32[8,2048]{1,0:T(8,128)}, f32[8,512]{1,0:T(8,128)}) custom-call(bf16[512,1024]{1,0:T(8,128)(2,1)} %get-tuple-element.12.a, bf16[512,1024]{1,0:T(8,128)(2,1)} %get-tuple-element.13.b, f32[8,2048]{1,0:T(8,128)} %get-tuple-element.14.p, f32[8,512]{1,0:T(8,128)} %get-tuple-element.15.q), custom_call_target="tpu_custom_call" | custom-call | tf_op jit(solution)/shard_map/finish/pallas_call | solution.py:714

commit v5 on v4

--- a/solution.py
+++ b/solution.py
@@ -16,7 +16,7 @@
 HALF_SCALE = 0.5 / math.sqrt(HD)
 MESH = pl.DeviceIdType.MESH
 NB = 5
-GROUPS = ((0, 2), (2, 1), (3, 2))
+GROUPS = ((0, 2), (2, 1), (3, 1), (4, 1))
 
 OWN_MOVES = (
     (0, 1, 0, (0, 1, 2, 3)),
@@ -652,6 +652,7 @@
     weight(4, normed_t, gh[:, 1536:2048])
     third(1)
     second(2)
+    second(3)
 
     @row_loop(256)
     def _(rows):
@@ -673,14 +674,17 @@
     output_out = pltpu.make_async_copy(output, output_hbm, out_sems.at[0])
     output_out.start()
     third(2)
+    third(3)
     fifth(0)
     fifth(1)
     fourth(2)
+    fourth(3)
     queries.drain()
     grads.drain()
     output_out.wait()
     tokens_out.wait()
     fifth(2)
+    fifth(3)
     for b in range(NB):
         result_copy(b).wait()
 
@@ -788,7 +792,7 @@
             dma((9,)), dma((10,)), dma((8,)), dma((8,)),
             dma((8,)), dma((10,)), dma((8,)), dma((8,)),
             dma((10,)), dma((8,)),
-            dma((NB,)), dma((NB,)), dma((3, 6)), dma((3, 6)), dma((3, 6)), dma((3, 3)),
+            dma((NB,)), dma((NB,)), dma((4, 6)), dma((4, 6)), dma((4, 6)), dma((4, 3)),
         ],
         compiler_params=pltpu.CompilerParams(
             collective_id=0, has_side_effects=True, vmem_limit_bytes=67043328),

time: 94.3 us -> 93.3 us (0.989)
  Pallas kernels: 93.2 us -> 92.2 us
    pallas_call x1, Pallas kernels: 90.8 us -> 89.7 us  [local(): pl.pallas_call(layer_kernel, name='layer', out_shape=(jax.ShapeDtypeStruc...]
where the time goes in v5:
time: 93.3 us; the launch traced here: 93 us
  Pallas kernels  92.2 us (99%)
    pallas_call x1, Pallas kernels, local(): pl.pallas_call(layer_kernel, name='layer', out_shape=(jax.ShapeDtypeStruc...  89.7 us
    pallas_call x1, Pallas kernels, finish(): pl.pallas_call(finish_kernel, name='finish', out_shape=(jax.ShapeDtypeStr...  2.46 us

profile of v5, /device:TPU:0, one launch (start us, length us, event | category | flops | bytes accessed | tf_op | source)
XLA Modules:
  0.0 93.0 jit_solution(15293141310245814215)
XLA Ops:
  0.6 89.7 %layer.1 = (bf16[512,1024]{1,0:T(8,128)(2,1)}, bf16[512,1024]{1,0:T(8,128)(2,1)}, f32[8,2048]{1,0:T(8,128)}, f32[8,512]{1,0:T(8,128)}) custom-call(bf16[512,1024]{1,0:T(8,128)(2,1)} %bitcast.3, s32[1,4096]{1,0:T(1,128)} %ids.1, bf16[1024,2048]{1,0:T(8,128)(2,1)} %w_in_hbm.1, bf16[512,1024]{1,0:T(8,128)(2,1)} %w_out_hbm.1, bf16[512,1024]{1,0:T(8,128)(2,1)} %bitcast.4), custom_call_target="tpu_custom_call" | custom-call | tf_op jit(solution)/shard_map/layer/pallas_call | solution.py:744
  90.4 2.5 %finish.1 = (bf16[1,512,1024]{2,1,0:T(8,128)(2,1)}, bf16[1,512,1024]{2,1,0:T(8,128)(2,1)}, f32[8,2048]{1,0:T(8,128)}, f32[8,512]{1,0:T(8,128)}) custom-call(bf16[512,1024]{1,0:T(8,128)(2,1)} %get-tuple-element.12.a, bf16[512,1024]{1,0:T(8,128)(2,1)} %get-tuple-element.13.b, f32[8,2048]{1,0:T(8,128)} %get-tuple-element.14.p, f32[8,512]{1,0:T(8,128)} %get-tuple-element.15.q), custom_call_target="tpu_custom_call" | custom-call | tf_op jit(solution)/shard_map/finish/pallas_call | solution.py:718
